TPU v7x, 256 devices: a whole 4x4x8 slice. The times are simulated.
256 devices in a mesh: rep: 32 (over y, z), hx: 8 (over x, core).
Axes of the slice: x: 4, y: 4, z: 8, core: 2. Of those that a mesh axis runs over, the one named last changes fastest.
Arguments:
- stream_in: bfloat16 [768, 6144], P(None, 'rep'), may hold values from -6 to 6
- query: bfloat16 [768, 6144], P('rep', 'hx'), may hold values from -240 to 240
- new_kv: bfloat16 [768, 2, 1024], P('rep', None, 'hx'), may hold values from -6 to 6
- cache: bfloat16 [768, 2, 128, 1024], P('rep', None, None, 'hx'), may hold values from -127 to 127, as said below
- precision: int32 [768, 4], P('rep'), may hold values from 0 to 1
- cache_scale: float32 [768, 2, 4, 8], P('rep', None, None, 'hx'), may hold values from 0.004 to 0.03
- lengths: int32 [768], P('rep'), may hold values from 0 to 128
- w_heads: bfloat16 [6144, 6144], P('hx', 'rep'), may hold values from -0.3125 to 0.3125
- norm_gain: float32 [6144], P('rep'), may hold values from 0.5 to 1.5
- w_router: bfloat16 [6144, 8], P('rep'), may hold values from -0.0390625 to 0.0390625
- expert_choice: int32 [768, 2], replicated, may hold values from 0 to 7, all different within a row; in each aligned block of 768 rows (0 to 767, 768 to 1535, ...) at most 384 rows name the same one
- w_in: bfloat16 [8, 6144, 2, 8192], P('hx', None, None, 'rep'), may hold values from -0.078125 to 0.078125
- w_down: bfloat16 [8, 8192, 6144], P('hx', 'rep'), may hold values from -0.0625 to 0.0625
- mig_dest: int32 [32], replicated, may hold values from 0 to 31, as said below
- mig_req: int32 [32], replicated, may hold values from 0 to 23
- mig_blocks: int32 [32], replicated, may hold values from 1 to 4
Outputs:
- mixed: bfloat16 [768, 6144], P(None, 'rep')
- arrived: bfloat16 [32, 2, 2, 128, 1024], P('rep', None, None, None, 'hx')
Inputs may be any that keep to these rules, and one draw needn't show every extreme that they name: `cache`: in blocks whose precision entry is 1, the stored values are whole numbers. `expert_choice`: each row names two different experts; over all 768 rows no expert is named by more than 384 rows, a bound that some block reaches. `mig_dest`: no replica names itself; no replica is named by more than 2 replicas, and one is named by exactly 2.
All inputs are finite; a program needn't handle non-finite values.
Results may differ from a plain program's by a relative error of at most 0.0065.
Values may be sent and summed in bfloat16 or wider, within the bound.
A program may use at most 128 MiB of HBM per device.

v0:
```python
import jax
import jax.numpy as jnp
from jax import lax
from jax.sharding import PartitionSpec as P

D = 6144
HEAD = 128
GROUP = 6
BLOCK_LEN = 32
IN_MOST = 2
CACHE = 128


EPSILON = 1e-05


def from_everyone(x, axis):
    copies = jnp.broadcast_to(x, (lax.axis_size(axis), *x.shape))
    return lax.all_to_all(copies, axis, split_axis=0, concat_axis=0, tiled=True)


def in_order(blocks, dim):
    blocks = jnp.moveaxis(blocks, 0, dim)
    lengths = blocks.shape
    return blocks.reshape(*lengths[:dim], lengths[dim] * lengths[dim + 1], *lengths[dim + 2 :])


def gather_directly(x, axis, dim):
    blocks = from_everyone(x, axis)
    return in_order(blocks, dim)


def taken_together(x, axis):
    return from_everyone(x, axis).sum(axis=0)


def over_copies(x, axis):
    everything = from_everyone(x, axis)
    return jnp.sum(everything.astype(jnp.float32), axis=0)


def block_factor(precision, cache_scale):
    factor = jnp.where(precision[:, None, :, None] == 1, cache_scale, 1.0)
    return jnp.repeat(factor, BLOCK_LEN, axis=2)


def attend(query, new_kv, cache, factor, lengths):
    rows = query.shape[0]
    heads_kv = new_kv.shape[2] // HEAD
    scale = HEAD ** (-0.5)
    queries = query.reshape(rows, heads_kv, GROUP, HEAD)
    keys = cache[:, 0].reshape(rows, CACHE, heads_kv, HEAD)
    values = cache[:, 1].reshape(rows, CACHE, heads_kv, HEAD)
    fresh = new_kv.reshape(rows, 2, heads_kv, HEAD)
    scores = jnp.einsum("rkgd,rpkd->rkgp", queries, keys, preferred_element_type=jnp.float32)
    scores = scores * jnp.transpose(factor[:, 0], (0, 2, 1))[:, :, None, :] * scale
    own = (
        jnp.einsum("rkgd,rkd->rkg", queries, fresh[:, 0], preferred_element_type=jnp.float32)
        * scale
    )
    live = jnp.arange(CACHE)[None, :] < lengths[:, None]
    scores = jnp.where(live[:, None, None, :], scores, -jnp.inf)
    top = jnp.maximum(jnp.max(scores, axis=3), own)
    weights = jnp.exp(scores - top[..., None])
    own_weight = jnp.exp(own - top)
    total = jnp.sum(weights, axis=3) + own_weight
    value_weight = (
        weights / total[..., None] * jnp.transpose(factor[:, 1], (0, 2, 1))[:, :, None, :]
    ).astype(jnp.bfloat16)
    own_prob = (own_weight / total).astype(jnp.bfloat16)
    result = jnp.einsum("rkgp,rpkd->rkgd", value_weight, values, preferred_element_type=jnp.float32)
    result = result + own_prob.astype(jnp.float32)[..., None] * fresh[:, 1][:, :, None, :].astype(
        jnp.float32
    )
    return result.reshape(rows, heads_kv * GROUP * HEAD).astype(jnp.bfloat16)


def local(
    stream_in,
    query,
    new_kv,
    cache,
    precision,
    cache_scale,
    lengths,
    w_heads,
    norm_gain,
    w_router,
    expert_choice,
    w_in,
    w_down,
    mig_dest,
    mig_req,
    mig_blocks,
):
    tokens = stream_in.shape[0]
    capacity = tokens // 2
    experts_all = w_router.shape[1]
    factor = block_factor(precision, cache_scale)
    attended = attend(query, new_kv, cache, factor, lengths)
    partial_value = jnp.dot(
        gather_directly(attended, "rep", 0), w_heads, preferred_element_type=jnp.float32
    )
    hidden_state = stream_in.astype(jnp.float32) + taken_together(partial_value, "hx")
    scaled = hidden_state * norm_gain[None, :]
    router_f32 = w_router.astype(jnp.float32)
    squares = taken_together(jnp.sum(hidden_state * hidden_state, axis=1), "rep")
    inverse = lax.rsqrt(squares / D + EPSILON)
    normed = scaled * inverse[:, None]
    logits = taken_together(jnp.dot(normed, router_f32, precision=lax.Precision.HIGHEST), "rep")
    onehot_choice = expert_choice[:, :, None] == jnp.arange(experts_all)[None, None, :]
    chosen = jnp.sum(jnp.where(onehot_choice, logits[:, None, :], 0.0), axis=2)
    peak = jnp.max(chosen, axis=1, keepdims=True)
    expo = jnp.exp(chosen - peak)
    gates = expo / jnp.sum(expo, axis=1, keepdims=True)
    u_rows = normed.astype(jnp.bfloat16)
    expert = lax.axis_index("hx")
    flat = expert_choice.reshape(-1)
    pair_token = jnp.arange(2 * tokens) // 2
    gate_flat = gates.reshape(-1)
    onehot = (flat[:, None] == jnp.arange(experts_all)[None, :]).astype(jnp.int32)
    rank = jnp.sum((jnp.cumsum(onehot, axis=0) - onehot) * onehot, axis=1)
    select = (flat[None, :] == expert) & (rank[None, :] == jnp.arange(capacity)[:, None])
    token_of_slot = jnp.sum(jnp.where(select, pair_token[None, :], 0), axis=1)
    live = jnp.any(select, axis=1)
    gate_of_slot = jnp.sum(jnp.where(select, gate_flat[None, :], 0.0), axis=1)
    match = (token_of_slot[:, None] == jnp.arange(tokens)[None, :]) & live[:, None]
    combine = jnp.where(match, gate_of_slot[:, None], 0.0)
    ff_local = w_in.shape[3]
    w_flat = w_in[0].reshape(D, 2 * ff_local)
    picked = jnp.where(live[:, None], u_rows[token_of_slot], jnp.zeros((), jnp.bfloat16))
    gate_up = jnp.dot(
        lax.all_gather(picked, "rep", axis=1, tiled=True),
        w_flat,
        preferred_element_type=jnp.float32,
    )
    act = (jax.nn.silu(gate_up[:, :ff_local]) * gate_up[:, ff_local:]).astype(jnp.bfloat16)
    down_rows = lax.all_to_all(w_down, "rep", split_axis=2, concat_axis=1, tiled=True)[0]
    expert_out = lax.dot_general(
        down_rows,
        lax.all_gather(act, "rep", axis=1, tiled=True),
        (((0,), (1,)), ((), ())),
        preferred_element_type=jnp.float32,
    )
    weighted = jnp.dot(expert_out, combine, precision=lax.Precision.HIGHEST)
    moe = over_copies(weighted.astype(jnp.bfloat16), "hx").astype(jnp.float32)
    mixed = (hidden_state + moe.T).astype(jnp.bfloat16)
    replica_id = lax.axis_index("rep")
    chosen_req = mig_req[replica_id]
    count = mig_blocks[replica_id]
    levels = lax.dynamic_index_in_dim(cache, chosen_req, 0, keepdims=False).astype(jnp.float32)
    scales = lax.dynamic_index_in_dim(factor, chosen_req, 0, keepdims=False)
    keep = jnp.arange(CACHE) < count * BLOCK_LEN
    outgoing = (
        jnp.where(keep[None, :, None], levels * scales, 0.0).astype(jnp.bfloat16).reshape(1, -1)
    )
    aimed = (mig_dest == replica_id).astype(jnp.int32)
    before = jnp.cumsum(aimed) - aimed
    slots = ((aimed[None, :] == 1) & (before[None, :] == jnp.arange(IN_MOST)[:, None])).astype(
        jnp.bfloat16
    )
    replicas = lax.axis_size("rep")
    target = mig_dest[replica_id]
    outbox = jnp.where(
        (jnp.arange(replicas) == target)[:, None], outgoing, jnp.zeros((), jnp.bfloat16)
    )
    received = lax.all_to_all(outbox, "rep", split_axis=0, concat_axis=0, tiled=True)
    arrived = jnp.dot(slots, received, preferred_element_type=jnp.float32)
    arrived = arrived.astype(jnp.bfloat16).reshape(1, IN_MOST, 2, CACHE, -1)
    return (mixed, arrived)


def solution(mesh):
    placed = (
        P(None, "rep"),
        P("rep", "hx"),
        P("rep", None, "hx"),
        P("rep", None, None, "hx"),
        P("rep", None),
        P("rep", None, None, "hx"),
        P("rep"),
        P("hx", "rep"),
        P("rep"),
        P("rep", None),
        P(),
        P("hx", None, None, "rep"),
        P("hx", "rep", None),
        P(),
        P(),
        P(),
    )
    return jax.shard_map(
        local,
        mesh=mesh,
        in_specs=placed,
        out_specs=(P(None, "rep"), P("rep", None, None, None, "hx")),
        check_vma=False,
    )
```

profile of v0, /device:TPU:1, one launch (start us, length us, event | category | flops | bytes accessed | tf_op | source)
XLA Modules:
  0.0 459.4 jit_solution(9098578894899218675)
XLA Ops:
  7.2 0.7 broadcast_compare_fusion.1
  7.9 0.7 broadcast_select_fusion.2
  8.9 0.8 reshape.308
  9.8 0.7 iota_compare_fusion.5
  10.5 0.7 copy.125
  11.4 1.7 fusion.56
  13.3 1.5 fusion.12
  15.0 43.0 %all_to_all.50 = bf16[32,24,768]{2,1,0:T(8,128)(2,1)S(1)} all-to-all(bf16[32,24,768]{2,1,0:T(8,128)(2,1)S(1)} %broadcast_in_dim.173), channel_id=1, replica_groups=mesh['rep'=32,'hx'=8] {'rep'}, dimensions={0} | all-to-all | bytes 2359296 | tf_op jit(solution)/shard_map/all_to_all | solution.py:19
  58.0 0.6 fusion.57
  58.6 2.6 broadcast_in_dim.174
  61.1 7.3 %all-to-all-start.1 = ((f32[8,768,192]{1,2,0:T(8,128)}), f32[8,768,192]{1,2,0:T(8,128)}, u32[]{:S(2)}, u32[]{:S(2)}) async-start(f32[8,768,192]{1,2,0:T(8,128)} %broadcast_in_dim.174), calls=%async_computation.1 | async-start | bytes 9437184 | tf_op jit(solution)/shard_map/all_to_all | solution.py:19
  68.6 0.2 eq.123
  68.8 0.2 broadcast_in_dim_reshape.2
  69.3 2.3 reduce-window.19
  71.6 0.3 slice_reduce_fusion
  72.2 0.6 select_reduce_fusion.1
  72.7 50.1 %all-to-all-done.1 = f32[8,768,192]{1,2,0:T(8,128)} async-done(((f32[8,768,192]{1,2,0:T(8,128)}), f32[8,768,192]{1,2,0:T(8,128)}, u32[]{:S(2)}, u32[]{:S(2)}) %all-to-all-start.1) | async-done | bytes 4718624 | tf_op jit(solution)/shard_map/all_to_all | solution.py:19
  122.8 2.7 reduce_sum.102
  125.5 0.3 copy.89
  126.0 0.7 broadcast_in_dim.176
  126.7 3.9 all-to-all-start.2
  130.6 0.4 fusion.1
  131.0 8.6 %all-to-all-done.2 = f32[32,1,768]{2,1,0:T(1,128)S(1)} async-done(((f32[32,1,768]{2,1,0:T(1,128)}), f32[32,1,768]{2,1,0:T(1,128)S(1)}, u32[]{:S(2)}, u32[]{:S(2)}) %all-to-all-start.2) | async-done | bytes 98336 | tf_op jit(solution)/shard_map/all_to_all | solution.py:19
  139.9 2.1 gather_fusion
  142.1 0.8 copy.93
  142.9 14.0 %copy.94 = bf16[1,256,6144]{1,0,2:T(2,128)(2,1)} copy(bf16[1,256,6144]{2,1,0:T(8,128)(2,1)} %param.28) | data formatting | bytes 6291456 | tf_op args[12]
  156.8 0.5 broadcast.197
  157.3 33.3 %reduce.10 = bf16[6144,256]{1,0:T(8,128)(2,1)} reduce(bf16[6144,1,256]{2,1,0:T(2,128)(2,1)} %bitcast.106, bf16[]{:T(256)} %broadcast.197), dimensions={1}, to_apply=%bitcast.88.reduce_sub_computation | reduce | bytes 6291458
  190.6 7.8 %reshape.333 = bf16[32,2,24576]{2,1,0:T(2,128)(2,1)} reshape(bf16[6144,256]{1,0:T(8,128)(2,1)} %reduce.10) | data formatting | bytes 6291456
  198.5 4.8 %all-to-all-start.3 = ((bf16[32,2,24576]{2,1,0:T(2,128)(2,1)}), bf16[32,2,24576]{2,1,0:T(2,128)(2,1)}, u32[]{:S(2)}, u32[]{:S(2)}) async-start(bf16[32,2,24576]{2,1,0:T(2,128)(2,1)} %reshape.333), calls=%async_computation.3 | async-start | bytes 6291456 | tf_op jit(solution)/shard_map/all_to_all | solution.py:138
  203.5 6.6 %copy.109 = bf16[768,8,2,256]{3,1,2,0:T(8,128)(2,1)} copy(bf16[768,8,2,256]{3,2,1,0:T(2,128)(2,1)} %bitcast.109) | data formatting | bytes 12582912
  210.1 28.7 %all-gather.3.cloned.1.call-done = bf16[384,6144]{0,1:T(8,128)(2,1)} async-done(((bf16[384,192]{0,1:T(8,128)(2,1)}), bf16[384,6144]{0,1:T(8,128)(2,1)}) %all-gather.3.cloned.1.call-update) | async-done | bytes 4718608 | tf_op jit(solution)/shard_map/all_gather | solution.py:133
  238.8 6.3 %fusion.58 = f32[384,512]{1,0:T(8,128)S(1)} fusion(bf16[384,6144]{0,1:T(8,128)(2,1)} %all-gather.3.cloned.1.call-done, bf16[6144,512]{1,0:T(8,128)(2,1)} %bitcast.105), kind=kOutput, calls=%fused_computation.109 | convolution fusion | flops 2415919104 | bytes 11796480 | tf_op jit(solution)/shard_map/dot_general | solution.py:132
  245.1 0.8 fusion.24
  245.9 0.7 dynamic_slice.19
  247.8 0.6 dynamic_slice.18
  248.5 0.6 dynamic_slice.17
  250.3 0.6 iota_compare_fusion.7
  250.9 0.9 constant_dynamic-slice_fusion.1
  252.0 0.6 fusion.18
  252.7 34.1 %all-to-all-done.3 = bf16[32,2,24576]{2,1,0:T(2,128)(2,1)} async-done(((bf16[32,2,24576]{2,1,0:T(2,128)(2,1)}), bf16[32,2,24576]{2,1,0:T(2,128)(2,1)}, u32[]{:S(2)}, u32[]{:S(2)}) %all-to-all-start.3) | async-done | bytes 3145760 | tf_op jit(solution)/shard_map/all_to_all | solution.py:138
  286.7 1.0 broadcast_in_dim.180
  287.7 6.6 %all-to-all-start.4 = ((f32[32,768,8]{1,2,0:T(8,128)}), f32[32,768,8]{1,2,0:T(8,128)S(1)}, u32[]{:S(2)}, u32[]{:S(2)}) async-start(f32[32,768,8]{1,2,0:T(8,128)} %broadcast_in_dim.180), calls=%async_computation.4 | async-start | bytes 1572864 | tf_op jit(solution)/shard_map/all_to_all | solution.py:19
  294.3 5.7 %broadcast_select_fusion = bf16[32,1,32768]{2,1,0:T(2,128)(2,1)} fusion(pred[32]{0:T(512)(128)(4,1)S(1)} %iota_compare_fusion.7, bf16[32768]{0:T(1024)(128)(2,1)S(1)} %fusion.28), kind=kLoop, calls=%fused_computation.2 | loop fusion | flops 1048576 | bytes 2162720 | tf_op jit(solution)/shard_map/jit(_where)/select_n | solution.py:164
  299.9 14.4 %reduce.11 = bf16[32,32768]{1,0:T(8,128)(2,1)} reduce(bf16[32,1,32768]{2,1,0:T(2,128)(2,1)} %broadcast_select_fusion, bf16[]{:T(256)} %broadcast.197), dimensions={1}, to_apply=%broadcast_select_fusion.reduce_sub_computation | reduce | bytes 4194306 | tf_op jit(solution)/shard_map/jit(_where)/select_n | solution.py:164
  314.4 4.5 reshape.335
  318.9 9.6 %all-to-all-start.6 = ((bf16[32,2,16384]{2,1,0:T(2,128)(2,1)}), bf16[32,2,16384]{2,1,0:T(2,128)(2,1)}, u32[]{:S(2)}, u32[]{:S(2)}) async-start(bf16[32,2,16384]{2,1,0:T(2,128)(2,1)} %reshape.335), calls=%async_computation.6 | async-start | bytes 4194304 | tf_op jit(solution)/shard_map/all_to_all | solution.py:167
  328.5 19.0 %reshape.334 = bf16[6144,1,256]{2,1,0:T(2,128)(2,1)} reshape(bf16[32,2,24576]{2,1,0:T(2,128)(2,1)} %all-to-all-done.3) | data formatting | bytes 6291456
  347.5 3.4 copy.102
  350.8 2.1 copy.110
  353.2 0.2 div.53
  353.5 0.6 select_reduce_fusion
  354.0 50.7 %all-gather.5.cloned.1.call-done = bf16[384,8192]{1,0:T(8,128)(2,1)} async-done(((bf16[384,256]{1,0:T(8,128)(2,1)}), bf16[384,8192]{1,0:T(8,128)(2,1)}) %all-gather.5.cloned.1.call-update) | async-done | bytes 6291472 | tf_op jit(solution)/shard_map/all_gather | solution.py:141
  404.7 5.9 %fusion.59 = f32[384,192]{0,1:T(8,128)S(1)} fusion(bf16[384,8192]{1,0:T(8,128)(2,1)} %all-gather.5.cloned.1.call-done, bf16[8192,192]{0,1:T(8,128)(2,1)} %bitcast.111), kind=kOutput, calls=%fused_computation.110 | convolution fusion | flops 1207959552 | bytes 9732096 | tf_op jit(solution)/shard_map/dot_general | solution.py:139
  410.6 1.4 convolution_convert_fusion.1
  412.0 1.6 broadcast_in_dim.187
  413.7 6.4 %all-to-all-start.5 = ((bf16[8,192,768]{2,1,0:T(8,128)(2,1)}), bf16[8,192,768]{2,1,0:T(8,128)(2,1)}, u32[]{:S(2)}, u32[]{:S(2)}) async-start(bf16[8,192,768]{2,1,0:T(8,128)(2,1)} %broadcast_in_dim.187), calls=%async_computation.5 | async-start | bytes 4718592 | tf_op jit(solution)/shard_map/all_to_all | solution.py:19
  420.4 10.5 %reshape.336 = bf16[32,1,32768]{2,1,0:T(2,128)(2,1)} reshape(bf16[32,2,16384]{2,1,0:T(2,128)(2,1)} %all-to-all-done.6) | data formatting | bytes 4194304
  430.8 4.5 fusion.7
  435.3 0.7 copy.111
  436.0 13.2 %all-to-all-done.5 = bf16[8,192,768]{2,1,0:T(8,128)(2,1)} async-done(((bf16[8,192,768]{2,1,0:T(8,128)(2,1)}), bf16[8,192,768]{2,1,0:T(8,128)(2,1)}, u32[]{:S(2)}, u32[]{:S(2)}) %all-to-all-start.5) | async-done | bytes 2359328 | tf_op jit(solution)/shard_map/all_to_all | solution.py:19
  449.2 2.1 convert_reduce_fusion
  451.3 0.3 copy.97
  451.7 0.9 copy.99
  (67 shorter events, 3.3 us)
Async XLA Ops:
  7.2 50.8 %copy-start = (bf16[768,192]{0,1:T(8,128)(2,1)S(1)}, bf16[768,192]{0,1:T(8,128)(2,1)}, u32[]{:S(2)}) copy-start(bf16[768,192]{0,1:T(8,128)(2,1)} %param.23) | copy-start | bytes 884740
  61.1 7.3 %copy-start.3 = (s32[768,2]{0,1:T(2,128)S(1)}, s32[768,2]{0,1:T(2,128)}, u32[]{:S(2)}) copy-start(s32[768,2]{0,1:T(2,128)} %param.26) | copy-start | bytes 18436
  61.1 7.9 %copy-start.2 = (bf16[768,192]{0,1:T(8,128)(2,1)S(1)}, bf16[768,192]{0,1:T(8,128)(2,1)}, u32[]{:S(2)}) copy-start(bf16[768,192]{0,1:T(8,128)(2,1)} %param.16) | copy-start | bytes 884740
  61.1 61.7 %all-to-all-start.1 = ((f32[8,768,192]{1,2,0:T(8,128)}), f32[8,768,192]{1,2,0:T(8,128)}, u32[]{:S(2)}, u32[]{:S(2)}) async-start(f32[8,768,192]{1,2,0:T(8,128)} %broadcast_in_dim.174), calls=%async_computation.1 | async-start | bytes 9437184 | tf_op jit(solution)/shard_map/all_to_all | solution.py:19
  125.5 14.1 %copy-start.5 = (f32[192]{0:T(256)S(1)}, f32[192]{0:T(256)}, u32[]{:S(2)}) copy-start(f32[192]{0:T(256)} %param.24) | copy-start | bytes 2308
  126.7 12.9 %all-to-all-start.2 = ((f32[32,1,768]{2,1,0:T(1,128)}), f32[32,1,768]{2,1,0:T(1,128)S(1)}, u32[]{:S(2)}, u32[]{:S(2)}) async-start(f32[32,1,768]{2,1,0:T(1,128)} %broadcast_in_dim.176), calls=%async_computation.2 | async-start | bytes 196608 | tf_op jit(solution)/shard_map/all_to_all | solution.py:19
  130.6 108.2 %all-gather.3.cloned.1.call-start = ((), (), s32[]{:S(2)}) async-start(), calls=%async_computation.7 | async-start | bytes 4866048 | tf_op jit(solution)/shard_map/all_gather | solution.py:133
  198.5 88.2 %all-to-all-start.3 = ((bf16[32,2,24576]{2,1,0:T(2,128)(2,1)}), bf16[32,2,24576]{2,1,0:T(2,128)(2,1)}, u32[]{:S(2)}, u32[]{:S(2)}) async-start(bf16[32,2,24576]{2,1,0:T(2,128)(2,1)} %reshape.333), calls=%async_computation.3 | async-start | bytes 6291456 | tf_op jit(solution)/shard_map/all_to_all | solution.py:138
  203.3 201.4 %all-gather.5.cloned.1.call-start = ((), (), s32[]{:S(2)}) async-start(), calls=%async_computation.8 | async-start | bytes 6488064 | tf_op jit(solution)/shard_map/all_gather | solution.py:141
  238.8 7.1 %copy-start.7 = (s32[32]{0:T(128)S(1)}, s32[32]{0:T(128)}, u32[]{:S(2)}) copy-start(s32[32]{0:T(128)} %param.30) | copy-start | bytes 388
  238.8 9.0 %copy-start.8 = (s32[32]{0:T(128)S(1)}, s32[32]{0:T(128)}, u32[]{:S(2)}) copy-start(s32[32]{0:T(128)} %param.31) | copy-start | bytes 388
  238.8 9.7 %copy-start.6 = (s32[32]{0:T(128)S(1)}, s32[32]{0:T(128)}, u32[]{:S(2)}) copy-start(s32[32]{0:T(128)} %param.29) | copy-start | bytes 388
  238.8 13.2 %copy-start.4 = (bf16[192,8]{0,1:T(8,128)(2,1)S(1)}, bf16[192,8]{0,1:T(8,128)(2,1)}, u32[]{:S(2)}) copy-start(bf16[192,8]{0,1:T(8,128)(2,1)} %param.25) | copy-start | bytes 9220
  287.7 31.2 %all-to-all-start.4 = ((f32[32,768,8]{1,2,0:T(8,128)}), f32[32,768,8]{1,2,0:T(8,128)S(1)}, u32[]{:S(2)}, u32[]{:S(2)}) async-start(f32[32,768,8]{1,2,0:T(8,128)} %broadcast_in_dim.180), calls=%async_computation.4 | async-start | bytes 1572864 | tf_op jit(solution)/shard_map/all_to_all | solution.py:19
  318.9 93.1 %all-to-all-start.6 = ((bf16[32,2,16384]{2,1,0:T(2,128)(2,1)}), bf16[32,2,16384]{2,1,0:T(2,128)(2,1)}, u32[]{:S(2)}, u32[]{:S(2)}) async-start(bf16[32,2,16384]{2,1,0:T(2,128)(2,1)} %reshape.335), calls=%async_computation.6 | async-start | bytes 4194304 | tf_op jit(solution)/shard_map/all_to_all | solution.py:167
  413.7 35.5 %all-to-all-start.5 = ((bf16[8,192,768]{2,1,0:T(8,128)(2,1)}), bf16[8,192,768]{2,1,0:T(8,128)(2,1)}, u32[]{:S(2)}, u32[]{:S(2)}) async-start(bf16[8,192,768]{2,1,0:T(8,128)(2,1)} %broadcast_in_dim.187), calls=%async_computation.5 | async-start | bytes 4718592 | tf_op jit(solution)/shard_map/all_to_all | solution.py:19
  449.2 3.4 copy-start.1
Sparse Core Ops, SparseCore 0:
  143.0 95.7 all-gather.2
  246.0 158.6 all-gather.4
where the time goes:
time: 462 us; the launch traced here: 459 us
  waiting for transfers between devices  185 us (40%)
  local copies, waits for them, and re-layouts  85.5 us (19%)
  other arithmetic  67.1 us (15%)
  blocking collectives  43 us (9%)
  starting transfers between devices  38.8 us (8%)
  matrix products  22.7 us (5%)
  between operations  17 us (4%)
    all_to_all x4, waiting for transfers between devices, from_everyone(): return lax.all_to_all(copies, axis, split_axis=0, concat_axis=0, tiled=True)  71.9 us
    unnamed x33, local copies, waits for them, and re-layouts  71 us
    all_gather x1, waiting for transfers between devices, local(): lax.all_gather(act, 'rep', axis=1, tiled=True)  50.7 us
    all_to_all x1, blocking collectives, from_everyone(): return lax.all_to_all(copies, axis, split_axis=0, concat_axis=0, tiled=True)  43 us
    all_to_all x1, waiting for transfers between devices, local(): lax.all_to_all(w_down, 'rep', split_axis=2, concat_axis=1, tiled=True)[0]  34.1 us
    unnamed x2, other arithmetic  33.4 us
    all_gather x1, waiting for transfers between devices, local(): lax.all_gather(picked, 'rep', axis=1, tiled=True)  28.7 us
    all_to_all x4, starting transfers between devices, from_everyone(): return lax.all_to_all(copies, axis, split_axis=0, concat_axis=0, tiled=True)  24.1 us
  transfers between devices with their start and end apart: 8, of which 6 were waited for; matrix products, arithmetic and copies ran while one was open for 33% of the time, Pallas kernels for 0%

commit v1 on v0

v1 whole, which is shorter than its diff:
```python
import functools

import jax
import jax.numpy as jnp
from jax import lax
from jax.experimental import pallas as pl
from jax.experimental.pallas import tpu as pltpu
from jax.sharding import PartitionSpec as P

D = 6144
HEAD = 128
GROUP = 6
BLOCK_LEN = 32
IN_MOST = 2
CACHE = 128
EPSILON = 1e-05

SIZES = {"y": 4, "z": 8, "x": 4, "c": 2}
PLANE = ("y", "z")
CHIPS = ("x", "c")


def coords():
    rep = lax.axis_index("rep")
    hx = lax.axis_index("hx")
    return {"y": rep // 8, "z": lax.rem(rep, 8), "x": hx // 2, "c": lax.rem(hx, 2)}


def device_at(at):
    return {"rep": at["y"] * 8 + at["z"], "hx": at["x"] * 2 + at["c"]}


def shifted(at, dim, step):
    n = SIZES[dim]
    moved = dict(at)
    moved[dim] = lax.rem(at[dim] + (step % n), n)
    return moved


def index_in(at, dims):
    if "y" in dims:
        return at["y"] * 8 + at["z"]
    return at["x"] * 2 + at["c"]


def ring_reach(n, flip):
    return (n // 2, n - 1 - n // 2) if flip % 2 == 0 else (n - 1 - n // 2, n // 2)


def gather_plan(na, nb, flip):
    events = []
    ra = ring_reach(na, flip)
    for oa in range(-ra[1], ra[0] + 1):
        rb = ring_reach(nb, oa + flip)
        for ob in range(-rb[1], rb[0] + 1):
            sends = []
            if ob == 0:
                for sign, limit in ((1, ra[0]), (-1, ra[1])):
                    if oa * sign >= 0 and abs(oa) < limit:
                        sends.append((0, sign))
            for sign, limit in ((1, rb[0]), (-1, rb[1])):
                if ob * sign >= 0 and abs(ob) < limit:
                    sends.append((1, sign))
            events.append((oa, ob, sends))
    return sorted(events, key=lambda e: (abs(e[0]) + abs(e[1]), abs(e[1])))


def enter(me, dims):
    barrier = pltpu.get_barrier_semaphore()
    count = 0
    for dim in dims:
        for step in (1, -1) if SIZES[dim] > 2 else (1,):
            pl.semaphore_signal(
                barrier,
                inc=1,
                device_id=device_at(shifted(me, dim, step)),
                device_id_type=pl.DeviceIdType.MESH,
            )
            count += 1
    pl.semaphore_wait(barrier, count)


def gather_body(items, greeted, n_in, *refs):
    ins, outs = refs[:n_in], refs[n_in : 2 * n_in]
    send_sem, recv_sem, own_sem = refs[2 * n_in :]
    me = coords()
    enter(me, greeted)
    todo, copies = [], []
    base_recv = 0
    for number, (which, part, dims, flip) in enumerate(items):
        a, b = dims
        plan = gather_plan(SIZES[a], SIZES[b], flip)
        for k, (oa, ob, sends) in enumerate(plan):
            todo.append((abs(oa) + abs(ob), number, oa, ob, sends))
        slots = {(oa, ob): base_recv + k for k, (oa, ob, _) in enumerate(plan)}
        items[number] = (which, part, dims, flip, slots)
        base_recv += len(plan)
    todo.sort(key=lambda e: e[0])
    sent = 0
    owned = []
    for hops, number, oa, ob, sends in todo:
        which, part, dims, flip, slots = items[number]
        origin = shifted(shifted(me, dims[0], -oa), dims[1], -ob)
        at = (index_in(origin, dims),) if part is None else (index_in(origin, dims), part)
        place = outs[which].at[at]
        if hops == 0:
            source = ins[which] if part is None else ins[which].at[part]
            own = pltpu.make_async_copy(source, place, own_sem.at[number])
            own.start()
            owned.append(own)
        else:
            source = place
            pltpu.make_async_remote_copy(
                src_ref=place,
                dst_ref=place,
                send_sem=send_sem.at[0],
                recv_sem=recv_sem.at[slots[(oa, ob)]],
                device_id=device_at(shifted(me, dims[0], 1)),
                device_id_type=pl.DeviceIdType.MESH,
            ).wait_recv()
        for along, sign in sends:
            to = (oa + sign, ob) if along == 0 else (oa, ob + sign)
            copy = pltpu.make_async_remote_copy(
                src_ref=source,
                dst_ref=place,
                send_sem=send_sem.at[sent],
                recv_sem=recv_sem.at[slots[to]],
                device_id=device_at(shifted(me, dims[along], sign)),
                device_id_type=pl.DeviceIdType.MESH,
            )
            copy.start()
            copies.append(copy)
            sent += 1
    for copy in copies:
        copy.wait_send()
    for own in owned:
        own.wait()


def gather_all(arrays, items, collective_id, name):
    greeted = []
    total = 0
    members = {}
    for which, part, dims, flip in items:
        members[which] = SIZES[dims[0]] * SIZES[dims[1]]
        total += members[which]
        greeted += [dim for dim in dims if dim not in greeted]
    return pl.pallas_call(
        lambda *refs: gather_body(list(items), greeted, len(arrays), *refs),
        out_shape=[
            jax.ShapeDtypeStruct((members[k], *x.shape), x.dtype) for k, x in enumerate(arrays)
        ],
        in_specs=[pl.BlockSpec(memory_space=pl.ANY)] * len(arrays),
        out_specs=[pl.BlockSpec(memory_space=pl.ANY)] * len(arrays),
        scratch_shapes=[
            pltpu.SemaphoreType.DMA((total,)),
            pltpu.SemaphoreType.DMA((total,)),
            pltpu.SemaphoreType.DMA((len(items),)),
        ],
        compiler_params=pltpu.CompilerParams(collective_id=collective_id, has_side_effects=True),
        name=name,
    )(*arrays)


def exchange_body(dim, x_ref, o_ref, send_sem, recv_sem):
    n = SIZES[dim]
    me = coords()
    barrier = pltpu.get_barrier_semaphore()
    for step in range(1, n):
        pl.semaphore_signal(
            barrier,
            inc=1,
            device_id=device_at(shifted(me, dim, step)),
            device_id_type=pl.DeviceIdType.MESH,
        )
    pl.semaphore_wait(barrier, n - 1)
    copies = []
    for step in sorted(range(1, n), key=lambda s: -min(s, n - s)):
        there = shifted(me, dim, step)
        copy = pltpu.make_async_remote_copy(
            src_ref=x_ref.at[there[dim]],
            dst_ref=o_ref.at[step - 1],
            send_sem=send_sem.at[step - 1],
            recv_sem=recv_sem.at[step - 1],
            device_id=device_at(there),
            device_id_type=pl.DeviceIdType.MESH,
        )
        copy.start()
        copies.append(copy)
    for copy in copies:
        copy.wait()


def exchange(x, dim, collective_id, name):
    n = SIZES[dim]
    return pl.pallas_call(
        functools.partial(exchange_body, dim),
        out_shape=jax.ShapeDtypeStruct((n - 1, *x.shape[1:]), x.dtype),
        in_specs=[pl.BlockSpec(memory_space=pl.ANY)],
        out_specs=pl.BlockSpec(memory_space=pl.ANY),
        scratch_shapes=[pltpu.SemaphoreType.DMA((n - 1,)), pltpu.SemaphoreType.DMA((n - 1,))],
        compiler_params=pltpu.CompilerParams(collective_id=collective_id, has_side_effects=True),
        name=name,
    )(x)


def block_factor(precision, cache_scale):
    factor = jnp.where(precision[:, None, :, None] == 1, cache_scale, 1.0)
    return jnp.repeat(factor, BLOCK_LEN, axis=2)


def attend(query, new_kv, cache, factor, lengths):
    rows = query.shape[0]
    heads_kv = new_kv.shape[2] // HEAD
    scale = HEAD ** (-0.5)
    queries = query.reshape(rows, heads_kv, GROUP, HEAD)
    keys = cache[:, 0].reshape(rows, CACHE, heads_kv, HEAD)
    values = cache[:, 1].reshape(rows, CACHE, heads_kv, HEAD)
    fresh = new_kv.reshape(rows, 2, heads_kv, HEAD)
    scores = jnp.einsum("rkgd,rpkd->rkgp", queries, keys, preferred_element_type=jnp.float32)
    scores = scores * jnp.transpose(factor[:, 0], (0, 2, 1))[:, :, None, :] * scale
    own = (
        jnp.einsum("rkgd,rkd->rkg", queries, fresh[:, 0], preferred_element_type=jnp.float32)
        * scale
    )
    live = jnp.arange(CACHE)[None, :] < lengths[:, None]
    scores = jnp.where(live[:, None, None, :], scores, -jnp.inf)
    top = jnp.maximum(jnp.max(scores, axis=3), own)
    weights = jnp.exp(scores - top[..., None])
    own_weight = jnp.exp(own - top)
    total = jnp.sum(weights, axis=3) + own_weight
    value_weight = (
        weights / total[..., None] * jnp.transpose(factor[:, 1], (0, 2, 1))[:, :, None, :]
    ).astype(jnp.bfloat16)
    own_prob = (own_weight / total).astype(jnp.bfloat16)
    result = jnp.einsum("rkgp,rpkd->rkgd", value_weight, values, preferred_element_type=jnp.float32)
    result = result + own_prob.astype(jnp.float32)[..., None] * fresh[:, 1][:, :, None, :].astype(
        jnp.float32
    )
    return result.reshape(rows, heads_kv * GROUP * HEAD).astype(jnp.bfloat16)


def contract_first(a, b, **kw):
    return lax.dot_general(
        a, b, (((0,), (0,)), ((), ())), preferred_element_type=jnp.float32, **kw
    )


def hand_off(cache, factor, mig_req, mig_blocks, replica_id):
    chosen_req = mig_req[replica_id]
    levels = lax.dynamic_index_in_dim(cache, chosen_req, 0, keepdims=False).astype(jnp.float32)
    scales = lax.dynamic_index_in_dim(factor, chosen_req, 0, keepdims=False)
    keep = jnp.arange(CACHE) < mig_blocks[replica_id] * BLOCK_LEN
    return jnp.where(keep[None, :, None], levels * scales, 0.0).astype(jnp.bfloat16)


def arrivals(everyones, mig_dest, replica_id):
    aimed = mig_dest == replica_id
    numbers = jnp.arange(mig_dest.shape[0])
    first = jnp.min(jnp.where(aimed, numbers, mig_dest.shape[0]))
    last = jnp.max(jnp.where(aimed, numbers, -1))
    rows = []
    for source, there in ((first, jnp.any(aimed)), (last, last > first)):
        row = lax.dynamic_index_in_dim(everyones, source, 0, keepdims=False)
        rows.append(jnp.where(there, row, jnp.zeros((), row.dtype)))
    return jnp.stack(rows)[None]


def local(
    stream_in,
    query,
    new_kv,
    cache,
    precision,
    cache_scale,
    lengths,
    w_heads,
    norm_gain,
    w_router,
    expert_choice,
    w_in,
    w_down,
    mig_dest,
    mig_req,
    mig_blocks,
):
    tokens, mine = stream_in.shape
    capacity = tokens // 2
    experts = w_router.shape[1]
    half = mine // 2
    ff = w_in.shape[3]
    replica_id = lax.axis_index("rep")
    expert = lax.axis_index("hx")
    y_id, z_id = replica_id // 8, lax.rem(replica_id, 8)

    factor = block_factor(precision, cache_scale)
    attended = attend(query, new_kv, cache, factor, lengths)
    split = attended.shape[1] // 2
    left, right = gather_all(
        [attended[:, :split], attended[:, split:]],
        [(0, None, ("z", "y"), 0), (1, None, ("y", "z"), 1)],
        1,
        "gather_attended",
    )
    part = lax.dot_general(
        w_heads[:split],
        left.reshape(tokens, split),
        (((0,), (1,)), ((), ())),
        preferred_element_type=jnp.float32,
    ) + lax.dot_general(
        w_heads[split:],
        right.reshape(tokens, split),
        (((0,), (1,)), ((), ())),
        preferred_element_type=jnp.float32,
    )
    outgoing = hand_off(cache, factor, mig_req, mig_blocks, replica_id)
    parts, everyones = gather_all(
        [part.astype(jnp.bfloat16).reshape(2, half, tokens), outgoing],
        [
            (0, 0, ("x", "c"), 0),
            (0, 1, ("x", "c"), 1),
            (1, 0, ("z", "y"), 0),
            (1, 1, ("y", "z"), 1),
        ],
        2,
        "gather_heads",
    )
    arrived = arrivals(everyones, mig_dest, replica_id)
    hidden = stream_in.T.astype(jnp.float32) + jnp.sum(
        parts.reshape(experts, mine, tokens).astype(jnp.float32), axis=0
    )

    ids = jnp.arange(experts)
    choice = expert_choice.T
    names = (choice[None, 0, :] == ids[:, None]) | (choice[None, 1, :] == ids[:, None])
    order = jnp.arange(tokens)
    earlier = (order[:, None] < order[None, :]).astype(jnp.bfloat16)
    rank = jnp.dot(
        names.astype(jnp.bfloat16), earlier, preferred_element_type=jnp.float32
    ).astype(jnp.int32)
    slot_of = jnp.where(names, rank, -1)
    my_slot = lax.dynamic_index_in_dim(slot_of, expert, 0, keepdims=False)
    pick = my_slot[:, None] == jnp.arange(capacity)[None, :]

    gained = hidden * norm_gain[:, None]
    u_slots = jnp.dot(
        gained.astype(jnp.bfloat16), pick.astype(jnp.bfloat16), preferred_element_type=jnp.float32
    ).astype(jnp.bfloat16)
    squares = jnp.sum(hidden * hidden, axis=0)
    logits = contract_first(
        w_router.astype(jnp.float32), gained, precision=lax.Precision.HIGHEST
    )
    first = jnp.sum(jnp.where(choice[None, 0, :] == ids[:, None], logits, 0.0), axis=0)
    second = jnp.sum(jnp.where(choice[None, 1, :] == ids[:, None], logits, 0.0), axis=0)
    ahead = jnp.where(choice[0] == expert, first - second, second - first)
    extra = jnp.concatenate(
        [squares[None], ahead[None], jnp.zeros((6, tokens), jnp.float32)], axis=0
    )
    extra_slots = jnp.dot(extra, pick.astype(jnp.float32), precision=lax.Precision.HIGHEST)
    u_all, extra_all = gather_all(
        [u_slots.reshape(2, half, capacity), extra_slots],
        [(0, 0, ("z", "y"), 0), (0, 1, ("y", "z"), 1), (1, None, ("y", "z"), 0)],
        3,
        "gather_rows",
    )
    sums = jnp.sum(extra_all, axis=0)
    inverse = lax.rsqrt(sums[0] / D + EPSILON)
    gate_of_slot = 1.0 / (1.0 + jnp.exp(-sums[1] * inverse))
    gate_up = contract_first(w_in[0].reshape(D, 2 * ff), u_all.reshape(D, capacity))
    gate_up = gate_up * inverse[None, :]
    act = (jax.nn.silu(gate_up[:ff]) * gate_up[ff:]).astype(jnp.bfloat16)
    out = contract_first(w_down[0], act).astype(jnp.bfloat16)

    out = out.reshape(4, 8, mine, capacity)
    from_y = exchange(out, "y", 4, "scatter_y")
    own = lax.dynamic_index_in_dim(out, y_id, 0, keepdims=False)
    out = own.astype(jnp.float32) + jnp.sum(from_y.astype(jnp.float32), axis=0)
    out = out.astype(jnp.bfloat16)
    from_z = exchange(out, "z", 5, "scatter_z")
    own = lax.dynamic_index_in_dim(out, z_id, 0, keepdims=False)
    out = own.astype(jnp.float32) + jnp.sum(from_z.astype(jnp.float32), axis=0)
    weighted = (out * gate_of_slot[None, :]).astype(jnp.bfloat16)
    (everyone,) = gather_all(
        [weighted.reshape(2, half, capacity)],
        [(0, 0, ("x", "c"), 0), (0, 1, ("x", "c"), 1)],
        6,
        "gather_experts",
    )
    place = (slot_of[:, None, :] == jnp.arange(capacity)[None, :, None]).astype(jnp.bfloat16)
    moe = lax.dot_general(
        everyone.reshape(experts, mine, capacity),
        place,
        (((0, 2), (0, 1)), ((), ())),
        preferred_element_type=jnp.float32,
    )
    mixed = (hidden + moe).astype(jnp.bfloat16).T
    return (mixed, arrived)


def solution(mesh):
    placed = (
        P(None, "rep"),
        P("rep", "hx"),
        P("rep", None, "hx"),
        P("rep", None, None, "hx"),
        P("rep", None),
        P("rep", None, None, "hx"),
        P("rep"),
        P("hx", "rep"),
        P("rep"),
        P("rep", None),
        P(),
        P("hx", None, None, "rep"),
        P("hx", "rep", None),
        P(),
        P(),
        P(),
    )
    return jax.shard_map(
        local,
        mesh=mesh,
        in_specs=placed,
        out_specs=(P(None, "rep"), P("rep", None, None, None, "hx")),
        check_vma=False,
    )
```

time: 462 us -> 270 us (0.58)
  Pallas kernels: 0 us -> 196 us
  waiting for transfers between devices: 185 us -> 0 us
  local copies, waits for them, and re-layouts: 85.5 us -> 22.7 us
  other arithmetic: 67.1 us -> 20.4 us
  blocking collectives: 43 us -> 0 us
  starting transfers between devices: 38.8 us -> 0 us
  between operations: 17 us -> 8.78 us
    pallas_call x0 -> x6, Pallas kernels: none -> 196 us  [the longest x4 110 us: gather_all(): pl.pallas_call(lambda *refs: gather_body(list(items), greeted, len(arrays...]
    all_to_all x6 -> x0, waiting for transfers between devices: 106 us -> none  [the longest x4 71.9 us: from_everyone(): return lax.all_to_all(copies, axis, split_axis=0, concat_axis=0, tiled=True)]
    all_gather x2 -> x0, waiting for transfers between devices: 79.3 us -> none  [the longest x1 50.7 us: local(): lax.all_gather(act, 'rep', axis=1, tiled=True)]
    unnamed x33 -> x37, local copies, waits for them, and re-layouts: 71 us -> 6.4 us
    all_to_all x1 -> x0, blocking collectives: 43 us -> none  [from_everyone(): return lax.all_to_all(copies, axis, split_axis=0, concat_axis=0, tiled=True)]
    all_to_all x6 -> x0, starting transfers between devices: 38.5 us -> none  [the longest x4 24.1 us: from_everyone(): return lax.all_to_all(copies, axis, split_axis=0, concat_axis=0, tiled=True)]
    unnamed x2 -> x0, other arithmetic: 33.4 us -> none
    select_n x5 -> x2, other arithmetic: 20.3 us -> 1.61 us  [the longest x1 1.6 us: arrivals(): rows.append(jnp.where(there, row, jnp.zeros((), row.dtype)))]
  transfers between devices with their start and end apart: 8 -> 0, of which waited for: 6 -> 0; matrix products, arithmetic and copies ran while one was open for 33% -> 0% of each run, Pallas kernels for 0% -> 0%
where the time goes in v1:
time: 270 us; the launch traced here: 268 us
  Pallas kernels  196 us (73%)
  local copies, waits for them, and re-layouts  22.7 us (8%)
  other arithmetic  20.4 us (8%)
  matrix products  20.4 us (8%)
  between operations  8.78 us (3%)
    pallas_call x4, Pallas kernels, gather_all(): pl.pallas_call(lambda *refs: gather_body(list(items), greeted, len(arrays...  110 us
    pallas_call x2, Pallas kernels, exchange(): pl.pallas_call(functools.partial(exchange_body, dim), out_shape=jax.Shape...  86.2 us
    dot_general x3, matrix products, contract_first(): lax.dot_general(a, b, (((0,), (0,)), ((), ())), preferred_element_type=jn...  6.63 us
    convert_element_type x1, local copies, waits for them, and re-layouts, local(): out = contract_first(w_down[0], act).astype(jnp.bfloat16)  6.62 us
    unnamed x37, local copies, waits for them, and re-layouts  6.4 us

profile of v1, /device:TPU:1, one launch (start us, length us, event | category | flops | bytes accessed | tf_op | source)
XLA Modules:
  0.0 268.4 jit_solution(629414797721052480)
XLA Ops:
  0.6 0.0 copy-start
  0.7 1.5 fusion.63
  2.2 1.2 dynamic_slice.33
  4.0 0.5 iota_compare_fusion.22
  4.6 1.2 dynamic_slice.34
  7.8 0.7 broadcast_compare_fusion
  8.5 0.6 pad.4.clone
  9.1 1.3 select_reduce_fusion.3
  15.6 1.3 iota_compare_fusion.21
  16.9 0.7 broadcast_select_fusion
  17.6 0.8 slice_reduce_fusion.1
  18.4 0.7 copy.38
  19.1 0.6 slice_bitcast_fusion.3
  19.7 0.7 copy.23
  20.4 0.2 fusion.18
  20.6 0.6 dynamic-slice_reduce_fusion
  21.2 0.0 copy-done.7
  21.2 0.8 reshape.177
  22.1 0.0 copy-start.6
  22.1 0.1 fusion.52
  22.2 0.5 copy-done.6
  22.7 0.8 broadcast_in_dim.96
  23.5 0.7 broadcast_in_dim.97
  24.2 0.7 constant_dynamic-slice_fusion.1
  25.0 0.7 slice_bitcast_fusion
  25.7 1.7 fusion.67
  27.4 0.2 fusion.39
  27.7 1.5 fusion.16
  29.2 0.6 fusion.65
  29.8 1.6 fusion.38.refs_1_
  31.4 24.9 %gather_attended.1 = (bf16[32,24,384]{2,1,0:T(8,128)(2,1)}, bf16[32,24,384]{2,1,0:T(8,128)(2,1)}) custom-call(bf16[24,384]{1,0:T(8,128)(2,1)} %get-tuple-element.27.refs_0_, bf16[24,384]{1,0:T(8,128)(2,1)} %get-tuple-element.26.refs_1_), custom_call_target="tpu_custom_call" | custom-call | tf_op jit(solution)/shard_map/gather_attended/pallas_call | solution.py:148
  56.3 0.0 copy-done.4
  56.3 1.4 fusion.35
  57.8 2.1 fusion.10
  59.9 34.8 %gather_heads.1 = (bf16[8,2,96,768]{3,2,1,0:T(8,128)(2,1)}, bf16[32,2,128,128]{3,2,1,0:T(8,128)(2,1)}) custom-call(bf16[2,96,768]{2,1,0:T(8,128)(2,1)} %bitcast.103, bf16[2,128,128]{2,1,0:T(8,128)(2,1)} %fusion.38.refs_1_), custom_call_target="tpu_custom_call" | custom-call | tf_op jit(solution)/shard_map/gather_heads/pallas_call | solution.py:148
  94.7 0.0 copy-start.8
  94.7 0.0 copy-start.10
  94.7 0.0 copy-start.12
  94.8 2.1 convert_reduce_fusion.1
  96.8 0.0 copy-start.9
  96.9 1.6 dynamic-slice_select_fusion.1
  98.5 0.7 maximum_bitcast_fusion
  99.1 0.1 multiply_reduce_fusion
  99.2 0.0 copy-done.8
  99.3 0.0 copy-done.10
  99.3 0.4 select_reduce_fusion.1
  99.7 1.1 fusion.13
  100.9 1.1 fusion.11.refs_1_
  102.0 37.1 %gather_rows.1 = (bf16[32,2,96,384]{3,2,1,0:T(8,128)(2,1)}, f32[32,8,384]{2,1,0:T(8,128)}) custom-call(bf16[2,96,384]{2,1,0:T(8,128)(2,1)} %bitcast.109, f32[8,384]{1,0:T(8,128)} %fusion.11.refs_1_), custom_call_target="tpu_custom_call" | custom-call | tf_op jit(solution)/shard_map/gather_rows/pallas_call | solution.py:148
  139.2 1.0 reduce_sum.85
  140.2 4.0 %copy.32 = bf16[768,8,2,256]{3,1,2,0:T(8,128)(2,1)S(1)} copy(bf16[768,8,2,256]{3,2,1,0:T(2,128)(2,1)} %bitcast.101) | data formatting | bytes 12582912
  144.3 0.1 copy-done.1
  144.4 2.6 fusion.6
  147.0 3.6 %fusion.1 = bf16[6144,384]{0,1:T(8,128)(2,1)} fusion(bf16[1,256,6144]{2,1,0:T(8,128)(2,1)S(1)} %copy-done, f32[512,384]{0,1:T(8,128)S(1)} %fusion.6), kind=kOutput, calls=%fused_computation.3 | convolution fusion | flops 1210908672 | bytes 8650752 | tf_op jit(solution)/shard_map/dot_general | solution.py:244
  150.6 6.6 %copy.26 = bf16[6144,384]{1,0:T(8,128)(2,1)} copy(bf16[6144,384]{0,1:T(8,128)(2,1)} %fusion.1) | data formatting | bytes 9437184 | tf_op jit(solution)/shard_map/convert_element_type | solution.py:372
  157.2 55.0 %scatter_y.1 = bf16[3,8,192,384]{3,2,1,0:T(8,128)(2,1)} custom-call(bf16[4,8,192,384]{3,2,1,0:T(8,128)(2,1)} %bitcast.98), custom_call_target="tpu_custom_call" | custom-call | tf_op jit(solution)/shard_map/scatter_y/pallas_call | solution.py:196
  212.3 2.8 %convert_reduce_fusion = f32[8,192,384]{2,1,0:T(8,128)S(1)} fusion(bf16[3,8,192,384]{3,2,1,0:T(8,128)(2,1)} %scatter_y.1), kind=kLoop, calls=%fused_computation.4 | loop fusion | flops 2949120 | bytes 5898240 | tf_op jit(solution)/shard_map/reduce_sum | solution.py:377
  215.1 1.5 fusion.4.x_ref
  216.7 1.0 copy-done.2
  217.7 31.2 %scatter_z.1 = bf16[7,192,384]{2,1,0:T(8,128)(2,1)} custom-call(bf16[8,192,384]{2,1,0:T(8,128)(2,1)} %copy-done.2), custom_call_target="tpu_custom_call" | custom-call | tf_op jit(solution)/shard_map/scatter_z/pallas_call | solution.py:196
  248.9 1.4 convert_reduce_fusion.2
  250.3 0.7 fusion.29.refs_0_
  251.0 13.2 %gather_experts.1 = bf16[8,2,96,384]{3,2,1,0:T(8,128)(2,1)} custom-call(bf16[2,96,384]{2,1,0:T(8,128)(2,1)} %fusion.29.refs_0_), custom_call_target="tpu_custom_call" | custom-call | tf_op jit(solution)/shard_map/gather_experts/pallas_call | solution.py:148
  264.2 4.3 %fusion.9 = bf16[768,192]{0,1:T(8,128)(2,1)} fusion(bf16[8,192,384]{2,1,0:T(8,128)(2,1)} %bitcast.104, s32[8,768]{1,0:T(8,128)S(1)} %copy-done.15, f32[768,192]{0,1:T(8,128)} %bitcast.102, bf16[768,192]{0,1:T(8,128)(2,1)} %param.16), kind=kOutput, calls=%fused_computation.18 | convolution fusion | flops 908918784 | bytes 2383872 | tf_op jit(solution)/shard_map/dot_general | solution.py:390
  (30 shorter events, 0.1 us)
Async XLA Ops:
  0.6 146.4 %copy-start = (bf16[1,256,6144]{2,1,0:T(8,128)(2,1)S(1)}, bf16[1,256,6144]{2,1,0:T(8,128)(2,1)}, u32[]{:S(2)}) copy-start(bf16[1,256,6144]{2,1,0:T(8,128)(2,1)} %param.28) | copy-start | bytes 9437188
  0.6 55.7 %copy-start.4 = (bf16[768,192]{0,1:T(8,128)(2,1)S(1)}, bf16[768,192]{0,1:T(8,128)(2,1)}, u32[]{:S(2)}) copy-start(bf16[768,192]{0,1:T(8,128)(2,1)} %param.23) | copy-start | bytes 884740
  18.4 2.9 %copy-start.7 = (s32[768]{0:T(1024)}, s32[768]{0:T(1024)S(1)}, u32[]{:S(2)}) copy-start(s32[768]{0:T(1024)S(1)} %get-tuple-element.19) | copy-start | bytes 9220
  20.6 1.6 copy-start.14
  22.1 0.6 copy-start.6
  24.2 5.6 %copy-start.13 = (pred[128]{0:T(512)(128)(4,1)S(1)}, pred[128]{0:T(512)(128)(4,1)}, u32[]{:S(2)}) copy-start(pred[128]{0:T(512)(128)(4,1)} %iota_compare_fusion.22) | copy-start | bytes 388
  59.9 39.2 %copy-start.5 = (bf16[768,192]{0,1:T(8,128)(2,1)S(1)}, bf16[768,192]{0,1:T(8,128)(2,1)}, u32[]{:S(2)}) copy-start(bf16[768,192]{0,1:T(8,128)(2,1)} %param.16) | copy-start | bytes 884740
  94.7 4.5 %copy-start.8 = (s32[768]{0:T(1024)S(1)}, s32[768]{0:T(1024)}, u32[]{:S(2)}) copy-start(s32[768]{0:T(1024)} %copy-done.7) | copy-start | bytes 9220
  94.7 4.5 %copy-start.10 = (bf16[192,8]{0,1:T(8,128)(2,1)S(1)}, bf16[192,8]{0,1:T(8,128)(2,1)}, u32[]{:S(2)}) copy-start(bf16[192,8]{0,1:T(8,128)(2,1)} %param.25) | copy-start | bytes 9220
  94.7 4.5 %copy-start.12 = (f32[192]{0:T(256)S(1)}, f32[192]{0:T(256)}, u32[]{:S(2)}) copy-start(f32[192]{0:T(256)} %param.24) | copy-start | bytes 2308
  94.8 5.0 %copy-start.11 = (s32[768]{0:T(1024)S(1)}, s32[768]{0:T(1024)}, u32[]{:S(2)}) copy-start(s32[768]{0:T(1024)} %dynamic-slice_reduce_fusion) | copy-start | bytes 9220
  96.8 4.0 %copy-start.3 = (f32[2,96,768]{2,1,0:T(8,128)}, f32[2,96,768]{2,1,0:T(8,128)S(1)}, u32[]{:S(2)}) copy-start(f32[2,96,768]{2,1,0:T(8,128)S(1)} %convert_reduce_fusion.1) | copy-start | bytes 1769476
  96.8 4.0 %copy-start.9 = (s32[768,2]{0,1:T(2,128)S(1)}, s32[768,2]{0,1:T(2,128)}, u32[]{:S(2)}) copy-start(s32[768,2]{0,1:T(2,128)} %param.26) | copy-start | bytes 18436
  96.8 4.0 %copy-start.16 = (f32[8]{0:T(128)S(1)}, f32[8]{0:T(128)}, u32[]{:S(2)}) copy-start(f32[8]{0:T(128)} %pad.4.clone) | copy-start | bytes 100
  140.2 4.2 %copy-start.1 = (bf16[32,2,96,384]{3,2,1,0:T(8,128)(2,1)S(1)}, bf16[32,2,96,384]{3,2,1,0:T(8,128)(2,1)}, u32[]{:S(2)}) copy-start(bf16[32,2,96,384]{3,2,1,0:T(8,128)(2,1)} %get-tuple-element.11) | copy-start | bytes 14155780
  216.6 1.0 copy-start.2
  217.7 46.5 %copy-start.15 = (s32[8,768]{1,0:T(8,128)S(1)}, s32[8,768]{1,0:T(8,128)}, u32[]{:S(2)}) copy-start(s32[8,768]{1,0:T(8,128)} %copy-done.14) | copy-start | bytes 73732

commit v2 on v1

--- a/solution.py
+++ b/solution.py
@@ -43,33 +43,74 @@
     return at["x"] * 2 + at["c"]
 
 
-def ring_reach(n, flip):
-    return (n // 2, n - 1 - n // 2) if flip % 2 == 0 else (n - 1 - n // 2, n // 2)
-
-
-def gather_plan(na, nb, flip):
+TREES = {
+    "ring": {
+        2: {0: (1,)},
+        4: {0: (1, -1), 1: (2,)},
+        8: {0: (1, -1), 1: (2,), 2: (3,), 3: (4,), -1: (-2,), -2: (-3,)},
+    },
+    "two": {
+        2: {0: (1,)},
+        4: {0: (1, -1, 2)},
+        8: {0: (1, -1, 2, -2), 2: (3, 4), -2: (-3,)},
+    },
+    "direct": {
+        2: {0: (1,)},
+        4: {0: (1, -1, 2)},
+        8: {0: (1, -1, 2, -2, 3, -3, 4)},
+    },
+}
+
+
+def tree_of(kind, n, flip):
+    sign = -1 if flip % 2 and n > 2 else 1
+    return {sign * o: tuple(sign * t for t in to) for o, to in TREES[kind][n].items()}
+
+
+def places_of(tree):
+    found = [0]
+    for o in found:
+        found += tree.get(o, ())
+    return found
+
+
+def depth_of(tree, o):
+    if o == 0:
+        return 0
+    return 1 + depth_of(tree, next(p for p, to in tree.items() if o in to))
+
+
+def gather_plan(dims, kinds, flip):
+    na, nb = SIZES[dims[0]], SIZES[dims[1]]
+    ta = tree_of(kinds[0], na, flip)
     events = []
-    ra = ring_reach(na, flip)
-    for oa in range(-ra[1], ra[0] + 1):
-        rb = ring_reach(nb, oa + flip)
-        for ob in range(-rb[1], rb[0] + 1):
+    for oa in places_of(ta):
+        tb = tree_of(kinds[1], nb, oa + flip)
+        for ob in places_of(tb):
             sends = []
             if ob == 0:
-                for sign, limit in ((1, ra[0]), (-1, ra[1])):
-                    if oa * sign >= 0 and abs(oa) < limit:
-                        sends.append((0, sign))
-            for sign, limit in ((1, rb[0]), (-1, rb[1])):
-                if ob * sign >= 0 and abs(ob) < limit:
-                    sends.append((1, sign))
-            events.append((oa, ob, sends))
-    return sorted(events, key=lambda e: (abs(e[0]) + abs(e[1]), abs(e[1])))
-
-
-def enter(me, dims):
+                sends += [(t, 0) for t in ta.get(oa, ())]
+            sends += [(oa, t) for t in tb.get(ob, ())]
+            cost = 3 * (depth_of(ta, oa) + depth_of(tb, ob)) + abs(oa) + abs(ob)
+            events.append((cost, oa, ob, sends))
+    return sorted(events, key=lambda e: e[0])
+
+
+def partners(dims, kinds):
+    found = {}
+    for dim, kind in zip(dims, kinds):
+        steps = found.setdefault(dim, set())
+        for o, to in TREES[kind][SIZES[dim]].items():
+            for t in to:
+                steps |= {(t - o) % SIZES[dim], (o - t) % SIZES[dim]}
+    return found
+
+
+def enter(me, steps):
     barrier = pltpu.get_barrier_semaphore()
     count = 0
-    for dim in dims:
-        for step in (1, -1) if SIZES[dim] > 2 else (1,):
+    for dim in sorted(steps):
+        for step in sorted(steps[dim]):
             pl.semaphore_signal(
                 barrier,
                 inc=1,
@@ -80,78 +121,75 @@
     pl.semaphore_wait(barrier, count)
 
 
-def gather_body(items, greeted, n_in, *refs):
+def remote(source, place, send_sem, recv_sem, there):
+    return pltpu.make_async_remote_copy(
+        src_ref=source,
+        dst_ref=place,
+        send_sem=send_sem,
+        recv_sem=recv_sem,
+        device_id=device_at(there),
+        device_id_type=pl.DeviceIdType.MESH,
+    )
+
+
+def gather_body(items, n_in, *refs):
     ins, outs = refs[:n_in], refs[n_in : 2 * n_in]
     send_sem, recv_sem, own_sem = refs[2 * n_in :]
     me = coords()
+    greeted = {}
+    for _, _, dims, kinds, _ in items:
+        for dim, steps in partners(dims, kinds).items():
+            greeted.setdefault(dim, set()).update(steps)
     enter(me, greeted)
-    todo, copies = [], []
-    base_recv = 0
-    for number, (which, part, dims, flip) in enumerate(items):
-        a, b = dims
-        plan = gather_plan(SIZES[a], SIZES[b], flip)
-        for k, (oa, ob, sends) in enumerate(plan):
-            todo.append((abs(oa) + abs(ob), number, oa, ob, sends))
-        slots = {(oa, ob): base_recv + k for k, (oa, ob, _) in enumerate(plan)}
-        items[number] = (which, part, dims, flip, slots)
-        base_recv += len(plan)
-    todo.sort(key=lambda e: e[0])
-    sent = 0
-    owned = []
-    for hops, number, oa, ob, sends in todo:
-        which, part, dims, flip, slots = items[number]
+    todo, slots, copies, owned = [], [], [], []
+    sems = 0
+    for number, (_, _, dims, kinds, flip) in enumerate(items):
+        plan = gather_plan(dims, kinds, flip)
+        todo += [(cost, number, oa, ob, sends) for cost, oa, ob, sends in plan]
+        slots.append({(oa, ob): sems + k for k, (_, oa, ob, _) in enumerate(plan)})
+        sems += len(plan)
+    for _, number, oa, ob, sends in sorted(todo, key=lambda e: e[0]):
+        which, part, dims, _, _ = items[number]
         origin = shifted(shifted(me, dims[0], -oa), dims[1], -ob)
         at = (index_in(origin, dims),) if part is None else (index_in(origin, dims), part)
         place = outs[which].at[at]
-        if hops == 0:
+        source = place
+        if (oa, ob) == (0, 0):
             source = ins[which] if part is None else ins[which].at[part]
+        else:
+            slot = slots[number][oa, ob]
+            remote(
+                place, place, send_sem.at[0], recv_sem.at[slot], shifted(me, dims[0], 1)
+            ).wait_recv()
+        for to in sends:
+            there = shifted(shifted(me, dims[0], to[0] - oa), dims[1], to[1] - ob)
+            slot = slots[number][to]
+            copy = remote(source, place, send_sem.at[slot], recv_sem.at[slot], there)
+            copy.start()
+            copies.append(copy)
+        if (oa, ob) == (0, 0):
             own = pltpu.make_async_copy(source, place, own_sem.at[number])
             own.start()
             owned.append(own)
-        else:
-            source = place
-            pltpu.make_async_remote_copy(
-                src_ref=place,
-                dst_ref=place,
-                send_sem=send_sem.at[0],
-                recv_sem=recv_sem.at[slots[(oa, ob)]],
-                device_id=device_at(shifted(me, dims[0], 1)),
-                device_id_type=pl.DeviceIdType.MESH,
-            ).wait_recv()
-        for along, sign in sends:
-            to = (oa + sign, ob) if along == 0 else (oa, ob + sign)
-            copy = pltpu.make_async_remote_copy(
-                src_ref=source,
-                dst_ref=place,
-                send_sem=send_sem.at[sent],
-                recv_sem=recv_sem.at[slots[to]],
-                device_id=device_at(shifted(me, dims[along], sign)),
-                device_id_type=pl.DeviceIdType.MESH,
-            )
-            copy.start()
-            copies.append(copy)
-            sent += 1
     for copy in copies:
         copy.wait_send()
     for own in owned:
         own.wait()
 
 
-def gather_all(arrays, items, collective_id, name):
-    greeted = []
+def gather_all(arrays, items, collective_id, name, space=pl.ANY):
     total = 0
     members = {}
-    for which, part, dims, flip in items:
+    for which, _, dims, _, _ in items:
         members[which] = SIZES[dims[0]] * SIZES[dims[1]]
         total += members[which]
-        greeted += [dim for dim in dims if dim not in greeted]
     return pl.pallas_call(
-        lambda *refs: gather_body(list(items), greeted, len(arrays), *refs),
+        functools.partial(gather_body, tuple(items), len(arrays)),
         out_shape=[
             jax.ShapeDtypeStruct((members[k], *x.shape), x.dtype) for k, x in enumerate(arrays)
         ],
-        in_specs=[pl.BlockSpec(memory_space=pl.ANY)] * len(arrays),
-        out_specs=[pl.BlockSpec(memory_space=pl.ANY)] * len(arrays),
+        in_specs=[pl.BlockSpec(memory_space=space)] * len(arrays),
+        out_specs=[pl.BlockSpec(memory_space=space)] * len(arrays),
         scratch_shapes=[
             pltpu.SemaphoreType.DMA((total,)),
             pltpu.SemaphoreType.DMA((total,)),
@@ -162,46 +200,132 @@
     )(*arrays)
 
 
-def exchange_body(dim, x_ref, o_ref, send_sem, recv_sem):
-    n = SIZES[dim]
+def dot_f32(a, b):
+    return jnp.dot(a, b, preferred_element_type=jnp.float32)
+
+
+def down_body(act_ref, w_ref, gate_ref, o_ref, p2, p1, pm, r1, fin, turned, tf, zr, *sems):
+    s1_send, s1_recv, s2_send, s2_recv, z_send, z_recv = sems
     me = coords()
-    barrier = pltpu.get_barrier_semaphore()
-    for step in range(1, n):
-        pl.semaphore_signal(
-            barrier,
-            inc=1,
-            device_id=device_at(shifted(me, dim, step)),
-            device_id_type=pl.DeviceIdType.MESH,
-        )
-    pl.semaphore_wait(barrier, n - 1)
+    enter(me, {"y": {1, 3}, "z": set(range(1, 8))})
+    up, down = shifted(me, "y", 1), shifted(me, "y", -1)
+    pair, odd = me["z"] // 2, lax.rem(me["z"], 2)
+    rows = act_ref.shape[0]
+    mid = rows // 2
+    wide = w_ref.shape[1] // 16
+    low, high = pl.ds(0, mid), pl.ds(mid, mid)
+    order = (2, 1, 3, 0)
+
+    def product(step, k):
+        there = lax.rem(me["y"] + step, 4)
+        start = there * (4 * wide) + lax.rem(pair + k, 4) * wide
+        return dot_f32(act_ref[...], w_ref[:, pl.ds(pl.multiple_of(start, 128), wide)])
+
     copies = []
-    for step in sorted(range(1, n), key=lambda s: -min(s, n - s)):
-        there = shifted(me, dim, step)
-        copy = pltpu.make_async_remote_copy(
-            src_ref=x_ref.at[there[dim]],
-            dst_ref=o_ref.at[step - 1],
-            send_sem=send_sem.at[step - 1],
-            recv_sem=recv_sem.at[step - 1],
-            device_id=device_at(there),
-            device_id_type=pl.DeviceIdType.MESH,
-        )
+
+    def send(source, place, ss, rs, there):
+        copy = remote(source, place, ss, rs, there)
         copy.start()
         copies.append(copy)
+        return copy
+
+    steps = {}
+    for k in order:
+        p2[k] = product(2, k).astype(p2.dtype)
+        a = send(p2.at[k, low], r1.at[k, 0], s1_send.at[k, 0], s1_recv.at[k, 0], up)
+        b = send(p2.at[k, high], r1.at[k, 1], s1_send.at[k, 1], s1_recv.at[k, 1], down)
+        steps[k] = (a, b)
+    lasts = {}
+    for k in order:
+        p1[k] = product(1, k).astype(p1.dtype)
+        c = send(p1.at[k, high], fin.at[k, 0, 1], s2_send.at[k, 0, 1], s2_recv.at[k, 0, 1], up)
+        pm[k] = product(3, k).astype(pm.dtype)
+        d = send(pm.at[k, low], fin.at[k, 1, 0], s2_send.at[k, 1, 0], s2_recv.at[k, 1, 0], down)
+        steps[k][0].wait_recv()
+        p1[k, low] = (p1[k, low].astype(jnp.float32) + r1[k, 0].astype(jnp.float32)).astype(p1.dtype)
+        e = send(p1.at[k, low], fin.at[k, 0, 0], s2_send.at[k, 0, 0], s2_recv.at[k, 0, 0], up)
+        steps[k][1].wait_recv()
+        pm[k, high] = (pm[k, high].astype(jnp.float32) + r1[k, 1].astype(jnp.float32)).astype(
+            pm.dtype
+        )
+        f = send(pm.at[k, high], fin.at[k, 1, 1], s2_send.at[k, 1, 1], s2_recv.at[k, 1, 1], down)
+        lasts[k] = (c, d, e, f)
+    for k in order:
+        whole = product(0, k)
+        for copy in lasts[k]:
+            copy.wait_recv()
+        whole = whole + jnp.concatenate(
+            [
+                fin[k, 0, 0].astype(jnp.float32) + fin[k, 1, 0].astype(jnp.float32),
+                fin[k, 0, 1].astype(jnp.float32) + fin[k, 1, 1].astype(jnp.float32),
+            ],
+            axis=0,
+        )
+        whole = whole.T
+        for e in range(2):
+            part = whole[e * (wide // 2) : (e + 1) * (wide // 2)]
+            turned[k, e] = part.astype(turned.dtype)
+            if k == 0:
+                tf[e] = part
+        first = 2 * lax.rem(pair + k, 4)
+        for e in range(2):
+            if k > 0:
+                there = dict(me, z=first + e)
+                send(
+                    turned.at[k, e],
+                    zr.at[2 * k + odd],
+                    z_send.at[2 * k + e],
+                    z_recv.at[2 * k + odd],
+                    there,
+                )
+        if k == 0:
+            there = dict(me, z=first + 1 - odd)
+            send(turned.at[0, 1 - odd], zr.at[odd], z_send.at[0], z_recv.at[odd], there)
+    total = tf[odd]
+    for k in order:
+        for e in range(2) if k > 0 else (0,):
+            slot = 2 * k + e if k > 0 else 1 - odd
+            remote(zr.at[slot], zr.at[slot], z_send.at[0], z_recv.at[slot], up).wait_recv()
+            total = total + zr[slot].astype(jnp.float32)
+    total = total * gate_ref[...]
+    n = o_ref.shape[1]
+    for h in range(2):
+        o_ref[h] = total[h * n : (h + 1) * n].astype(o_ref.dtype)
     for copy in copies:
-        copy.wait()
-
-
-def exchange(x, dim, collective_id, name):
-    n = SIZES[dim]
+        copy.wait_send()
+
+
+def down_and_scatter(act, w_down, gate, collective_id):
+    rows, depth = act.shape
+    width = w_down.shape[1] // 16
+    vmem = pl.BlockSpec(memory_space=pltpu.VMEM)
+    kind = act.dtype
     return pl.pallas_call(
-        functools.partial(exchange_body, dim),
-        out_shape=jax.ShapeDtypeStruct((n - 1, *x.shape[1:]), x.dtype),
-        in_specs=[pl.BlockSpec(memory_space=pl.ANY)],
-        out_specs=pl.BlockSpec(memory_space=pl.ANY),
-        scratch_shapes=[pltpu.SemaphoreType.DMA((n - 1,)), pltpu.SemaphoreType.DMA((n - 1,))],
-        compiler_params=pltpu.CompilerParams(collective_id=collective_id, has_side_effects=True),
-        name=name,
-    )(x)
+        down_body,
+        out_shape=jax.ShapeDtypeStruct((2, width // 4, rows), kind),
+        in_specs=[vmem] * 3,
+        out_specs=vmem,
+        scratch_shapes=[
+            pltpu.VMEM((4, rows, width), kind),
+            pltpu.VMEM((4, rows, width), kind),
+            pltpu.VMEM((4, rows, width), kind),
+            pltpu.VMEM((4, 2, rows // 2, width), kind),
+            pltpu.VMEM((4, 2, 2, rows // 2, width), kind),
+            pltpu.VMEM((4, 2, width // 2, rows), kind),
+            pltpu.VMEM((2, width // 2, rows), jnp.float32),
+            pltpu.VMEM((8, width // 2, rows), kind),
+            pltpu.SemaphoreType.DMA((4, 2)),
+            pltpu.SemaphoreType.DMA((4, 2)),
+            pltpu.SemaphoreType.DMA((4, 2, 2)),
+            pltpu.SemaphoreType.DMA((4, 2, 2)),
+            pltpu.SemaphoreType.DMA((8,)),
+            pltpu.SemaphoreType.DMA((8,)),
+        ],
+        compiler_params=pltpu.CompilerParams(
+            collective_id=collective_id, has_side_effects=True, vmem_limit_bytes=48 * 2**20
+        ),
+        name="down_scatter",
+    )(act, w_down, gate)
 
 
 def block_factor(precision, cache_scale):
@@ -291,14 +415,16 @@
     ff = w_in.shape[3]
     replica_id = lax.axis_index("rep")
     expert = lax.axis_index("hx")
-    y_id, z_id = replica_id // 8, lax.rem(replica_id, 8)
 
     factor = block_factor(precision, cache_scale)
     attended = attend(query, new_kv, cache, factor, lengths)
     split = attended.shape[1] // 2
     left, right = gather_all(
         [attended[:, :split], attended[:, split:]],
-        [(0, None, ("z", "y"), 0), (1, None, ("y", "z"), 1)],
+        [
+            (0, None, ("z", "y"), ("two", "two"), 0),
+            (1, None, ("y", "z"), ("two", "two"), 1),
+        ],
         1,
         "gather_attended",
     )
@@ -317,10 +443,10 @@
     parts, everyones = gather_all(
         [part.astype(jnp.bfloat16).reshape(2, half, tokens), outgoing],
         [
-            (0, 0, ("x", "c"), 0),
-            (0, 1, ("x", "c"), 1),
-            (1, 0, ("z", "y"), 0),
-            (1, 1, ("y", "z"), 1),
+            (0, 0, ("x", "c"), ("ring", "ring"), 0),
+            (0, 1, ("x", "c"), ("ring", "ring"), 1),
+            (1, 0, ("z", "y"), ("ring", "ring"), 0),
+            (1, 1, ("y", "z"), ("ring", "ring"), 1),
         ],
         2,
         "gather_heads",
@@ -359,7 +485,11 @@
     extra_slots = jnp.dot(extra, pick.astype(jnp.float32), precision=lax.Precision.HIGHEST)
     u_all, extra_all = gather_all(
         [u_slots.reshape(2, half, capacity), extra_slots],
-        [(0, 0, ("z", "y"), 0), (0, 1, ("y", "z"), 1), (1, None, ("y", "z"), 0)],
+        [
+            (0, 0, ("z", "y"), ("ring", "ring"), 0),
+            (0, 1, ("y", "z"), ("ring", "ring"), 1),
+            (1, None, ("y", "z"), ("ring", "ring"), 0),
+        ],
         3,
         "gather_rows",
     )
@@ -369,21 +499,14 @@
     gate_up = contract_first(w_in[0].reshape(D, 2 * ff), u_all.reshape(D, capacity))
     gate_up = gate_up * inverse[None, :]
     act = (jax.nn.silu(gate_up[:ff]) * gate_up[ff:]).astype(jnp.bfloat16)
-    out = contract_first(w_down[0], act).astype(jnp.bfloat16)
-
-    out = out.reshape(4, 8, mine, capacity)
-    from_y = exchange(out, "y", 4, "scatter_y")
-    own = lax.dynamic_index_in_dim(out, y_id, 0, keepdims=False)
-    out = own.astype(jnp.float32) + jnp.sum(from_y.astype(jnp.float32), axis=0)
-    out = out.astype(jnp.bfloat16)
-    from_z = exchange(out, "z", 5, "scatter_z")
-    own = lax.dynamic_index_in_dim(out, z_id, 0, keepdims=False)
-    out = own.astype(jnp.float32) + jnp.sum(from_z.astype(jnp.float32), axis=0)
-    weighted = (out * gate_of_slot[None, :]).astype(jnp.bfloat16)
+    weighted = down_and_scatter(act.T, w_down[0], gate_of_slot[None], 4)
     (everyone,) = gather_all(
-        [weighted.reshape(2, half, capacity)],
-        [(0, 0, ("x", "c"), 0), (0, 1, ("x", "c"), 1)],
-        6,
+        [weighted],
+        [
+            (0, 0, ("x", "c"), ("ring", "ring"), 0),
+            (0, 1, ("x", "c"), ("ring", "ring"), 1),
+        ],
+        5,
         "gather_experts",
     )
     place = (slot_of[:, None, :] == jnp.arange(capacity)[None, :, None]).astype(jnp.bfloat16)

time: 270 us -> 206 us (0.76)
  Pallas kernels: 196 us -> 159 us
  local copies, waits for them, and re-layouts: 22.7 us -> 10.6 us
  other arithmetic: 20.4 us -> 11.4 us
  matrix products: 20.4 us -> 15.4 us
    pallas_call x6 -> x5, Pallas kernels: 196 us -> 159 us  [the longest x4 109 us: gather_all(): pl.pallas_call(functools.partial(gather_body, tuple(items), len(arrays)),...]
    convert_element_type x1 -> x0, local copies, waits for them, and re-layouts: 6.62 us -> none  [local(): out = contract_first(w_down[0], act).astype(jnp.bfloat16)]
    reduce_sum x2 -> x0, other arithmetic: 4.2 us -> none  [the longest x1 2.82 us: local(): out = own.astype(jnp.float32) + jnp.sum(from_y.astype(jnp.float32), axis=0)]
    dot_general x3 -> x2, matrix products: 6.63 us -> 3.04 us  [contract_first(): lax.dot_general(a, b, (((0,), (0,)), ((), ())), preferred_element_type=jn...]
    unnamed x37 -> x23, local copies, waits for them, and re-layouts: 6.4 us -> 5.46 us
where the time goes in v2:
time: 206 us; the launch traced here: 205 us
  Pallas kernels  159 us (77%)
  matrix products  15.4 us (7%)
  other arithmetic  11.4 us (6%)
  local copies, waits for them, and re-layouts  10.6 us (5%)
  between operations  8.73 us (4%)
    pallas_call x4, Pallas kernels, gather_all(): pl.pallas_call(functools.partial(gather_body, tuple(items), len(arrays)),...  109 us
    pallas_call x1, Pallas kernels, down_and_scatter(): pl.pallas_call(down_body, out_shape=jax.ShapeDtypeStruct((2, width // 4,...  50.1 us
    unnamed x23, local copies, waits for them, and re-layouts  5.46 us

profile of v2, /device:TPU:1, one launch (start us, length us, event | category | flops | bytes accessed | tf_op | source)
XLA Modules:
  0.0 205.4 jit_solution(17510272138645088428)
XLA Ops:
  0.6 0.0 copy-start
  0.6 0.0 copy-start.3
  0.7 0.0 copy-start.4
  0.7 1.4 fusion.56
  2.1 1.2 dynamic_slice.25
  4.0 1.2 dynamic_slice.26
  7.2 0.7 broadcast_compare_fusion
  7.9 0.1 pad.4.clone
  8.0 1.3 select_reduce_fusion.3
  14.4 0.7 iota_compare_fusion.21
  15.2 0.7 broadcast_select_fusion
  15.9 0.8 slice_reduce_fusion.1
  16.7 0.7 copy.36
  17.4 0.1 copy.22
  17.5 0.2 fusion.15
  17.7 0.8 reshape.162
  18.6 0.1 fusion.46
  18.7 0.1 broadcast_in_dim.96
  18.8 0.1 broadcast_in_dim.97
  19.0 1.7 fusion.60
  20.7 0.2 fusion.33
  20.9 0.0 copy-done.3
  20.9 0.4 fusion.13
  21.3 0.6 fusion.58
  22.0 0.7 fusion.32.refs_1_
  22.7 21.9 %gather_attended.1 = (bf16[32,24,384]{2,1,0:T(8,128)(2,1)}, bf16[32,24,384]{2,1,0:T(8,128)(2,1)}) custom-call(bf16[24,384]{1,0:T(8,128)(2,1)} %get-tuple-element.25.refs_0_, bf16[24,384]{1,0:T(8,128)(2,1)} %get-tuple-element.24.refs_1_), custom_call_target="tpu_custom_call" | custom-call | tf_op jit(solution)/shard_map/gather_attended/pallas_call | solution.py:186
  44.6 0.0 copy-done.4
  44.6 1.4 fusion.29
  46.0 0.0 copy-start.5
  46.0 2.2 %fusion.7 = bf16[768,192]{0,1:T(8,128)(2,1)} fusion(f32[768,192]{0,1:T(8,128)S(1)} %fusion.29, bf16[768,384]{1,0:T(8,128)(2,1)} %bitcast.97, bf16[768,192]{0,1:T(8,128)(2,1)S(1)} %copy-done.4), kind=kOutput, calls=%fused_computation.12 | convolution fusion | flops 113541120 | bytes 1622016 | tf_op jit(solution)/shard_map/dot_general | solution.py:436
  48.2 33.2 %gather_heads.1 = (bf16[8,2,96,768]{3,2,1,0:T(8,128)(2,1)}, bf16[32,2,128,128]{3,2,1,0:T(8,128)(2,1)}) custom-call(bf16[2,96,768]{2,1,0:T(8,128)(2,1)} %bitcast.95, bf16[2,128,128]{2,1,0:T(8,128)(2,1)} %fusion.32.refs_1_), custom_call_target="tpu_custom_call" | custom-call | tf_op jit(solution)/shard_map/gather_heads/pallas_call | solution.py:186
  81.5 0.0 copy-start.7
  81.5 2.0 convert_reduce_fusion
  83.5 0.0 copy-start.6
  83.5 1.5 dynamic-slice_select_fusion.1
  85.1 0.7 maximum_bitcast_fusion
  85.7 0.0 copy-done.5
  85.7 0.1 multiply_reduce_fusion
  85.8 0.0 copy-done
  85.9 0.0 copy-done.7
  85.9 0.4 select_reduce_fusion.1
  86.3 1.1 fusion.10
  87.4 0.0 copy-done.6
  87.4 1.1 fusion.8.refs_1_
  88.6 36.9 %gather_rows.1 = (bf16[32,2,96,384]{3,2,1,0:T(8,128)(2,1)}, f32[32,8,384]{2,1,0:T(8,128)}) custom-call(bf16[2,96,384]{2,1,0:T(8,128)(2,1)} %bitcast.99, f32[8,384]{1,0:T(8,128)} %fusion.8.refs_1_), custom_call_target="tpu_custom_call" | custom-call | tf_op jit(solution)/shard_map/gather_rows/pallas_call | solution.py:186
  125.5 0.0 slice-start
  125.5 1.1 reduce_sum.65
  126.7 0.0 slice-start.1
  126.7 4.0 %copy.30 = bf16[768,8,2,256]{3,1,2,0:T(8,128)(2,1)S(1)} copy(bf16[768,8,2,256]{3,2,1,0:T(2,128)(2,1)} %bitcast.93) | data formatting | bytes 12582912
  130.7 0.0 slice-done
  130.7 0.0 slice-done.1
  130.7 0.0 copy-start.1
  130.7 2.6 %fusion.3 = f32[512,384]{0,1:T(8,128)S(1)} fusion(bf16[6144,384]{1,0:T(8,128)(2,1)S(1)} %bitcast.92, bf16[6144,512]{1,0:T(8,128)(2,1)S(1)} %bitcast.89, f32[384]{0:T(512)S(1)} %get-tuple-element.31), kind=kOutput, calls=%fused_computation.7 | convolution fusion | flops 2416115712 | bytes 11798016 | tf_op jit(solution)/shard_map/dot_general | solution.py:368
  133.4 0.1 fusion.27.act_ref
  133.5 0.0 copy-done.1
  133.5 50.1 %down_scatter.1.refs_0_ = bf16[2,96,384]{2,1,0:T(8,128)(2,1)S(1)} custom-call(bf16[384,256]{1,0:T(8,128)(2,1)S(1)} %fusion.27.act_ref, bf16[256,6144]{1,0:T(8,128)(2,1)S(1)} %bitcast.88, f32[1,384]{1,0:T(1,128)S(1)} %get-tuple-element.30.gate_ref), custom_call_target="tpu_custom_call" | custom-call | tf_op jit(solution)/shard_map/down_scatter/pallas_call | solution.py:303
  183.6 0.0 copy-start.2
  183.6 0.7 copy-done.2
  184.3 17.1 %gather_experts.1 = bf16[8,2,96,384]{3,2,1,0:T(8,128)(2,1)} custom-call(bf16[2,96,384]{2,1,0:T(8,128)(2,1)} %copy-done.2), custom_call_target="tpu_custom_call" | custom-call | tf_op jit(solution)/shard_map/gather_experts/pallas_call | solution.py:186
  201.4 4.0 %fusion.6 = bf16[768,192]{0,1:T(8,128)(2,1)} fusion(bf16[8,192,384]{2,1,0:T(8,128)(2,1)} %bitcast.96, s32[8,768]{1,0:T(8,128)S(1)} %fusion.15, f32[768,192]{0,1:T(8,128)S(1)} %bitcast.94, bf16[768,192]{0,1:T(8,128)(2,1)S(1)} %copy-done.5), kind=kOutput, calls=%fused_computation.11 | convolution fusion | flops 908918784 | bytes 2383872 | tf_op jit(solution)/shard_map/dot_general | solution.py:513
  (14 shorter events, 0.1 us)
Async XLA Ops:
  0.6 85.2 %copy-start = (bf16[192,8]{0,1:T(8,128)(2,1)S(1)}, bf16[192,8]{0,1:T(8,128)(2,1)}, u32[]{:S(2)}) copy-start(bf16[192,8]{0,1:T(8,128)(2,1)} %param.25) | copy-start | bytes 9220
  0.6 20.3 %copy-start.3 = (bf16[24,2,128,128]{3,2,1,0:T(8,128)(2,1)S(1)}, bf16[24,2,128,128]{3,2,1,0:T(8,128)(2,1)}, u32[]{:S(2)}) copy-start(bf16[24,2,128,128]{3,2,1,0:T(8,128)(2,1)} %param.19) | copy-start | bytes 4718596
  0.7 43.9 %copy-start.4 = (bf16[768,192]{0,1:T(8,128)(2,1)S(1)}, bf16[768,192]{0,1:T(8,128)(2,1)}, u32[]{:S(2)}) copy-start(bf16[768,192]{0,1:T(8,128)(2,1)} %param.23) | copy-start | bytes 884740
  46.0 39.7 %copy-start.5 = (bf16[768,192]{0,1:T(8,128)(2,1)S(1)}, bf16[768,192]{0,1:T(8,128)(2,1)}, u32[]{:S(2)}) copy-start(bf16[768,192]{0,1:T(8,128)(2,1)} %param.16) | copy-start | bytes 884740
  81.5 4.4 %copy-start.7 = (f32[192]{0:T(256)S(1)}, f32[192]{0:T(256)}, u32[]{:S(2)}) copy-start(f32[192]{0:T(256)} %param.24) | copy-start | bytes 2308
  83.5 3.9 %copy-start.6 = (s32[768,2]{0,1:T(2,128)S(1)}, s32[768,2]{0,1:T(2,128)}, u32[]{:S(2)}) copy-start(s32[768,2]{0,1:T(2,128)} %param.26) | copy-start | bytes 18436
  125.5 5.2 %slice-start = ((s8[4718592]{0:T(1024)(128)(4,1)}), s8[524288]{0:T(1024)(128)(4,1)S(1)}, s32[]{:S(2)}) async-start(s8[4718592]{0:T(1024)(128)(4,1)} %bitcast.90), calls=%async_computation | async-start | bytes 1048576
  126.7 4.1 %slice-start.1 = ((s8[4718592]{0:T(1024)(128)(4,1)}), s8[4194304]{0:T(1024)(128)(4,1)S(1)}, s32[]{:S(2)}) async-start(s8[4718592]{0:T(1024)(128)(4,1)} %bitcast.90), calls=%async_computation.1 | async-start | bytes 8388608
  130.7 2.8 %copy-start.1 = (bf16[1,256,6144]{2,1,0:T(8,128)(2,1)S(1)}, bf16[1,256,6144]{2,1,0:T(8,128)(2,1)}, u32[]{:S(2)}) copy-start(bf16[1,256,6144]{2,1,0:T(8,128)(2,1)} %param.28) | copy-start | bytes 9437188
  183.6 0.7 copy-start.2

commit v3 on v2

v3 whole, which is shorter than its diff:
```python
import functools

import jax
import jax.numpy as jnp
from jax import lax
from jax.experimental import pallas as pl
from jax.experimental.pallas import tpu as pltpu
from jax.sharding import PartitionSpec as P

D = 6144
HEAD = 128
GROUP = 6
BLOCK_LEN = 32
IN_MOST = 2
CACHE = 128
EPSILON = 1e-05

SIZES = {"y": 4, "z": 8, "x": 4, "c": 2}
PLANE = ("y", "z")
CHIPS = ("x", "c")


def coords():
    rep = lax.axis_index("rep")
    hx = lax.axis_index("hx")
    return {"y": rep // 8, "z": lax.rem(rep, 8), "x": hx // 2, "c": lax.rem(hx, 2)}


def device_at(at):
    return {"rep": at["y"] * 8 + at["z"], "hx": at["x"] * 2 + at["c"]}


def shifted(at, dim, step):
    n = SIZES[dim]
    moved = dict(at)
    moved[dim] = lax.rem(at[dim] + (step % n), n)
    return moved


def index_in(at, dims):
    if "y" in dims:
        return at["y"] * 8 + at["z"]
    return at["x"] * 2 + at["c"]


TREES = {
    "ring": {
        2: {0: (1,)},
        4: {0: (1, -1), 1: (2,)},
        8: {0: (1, -1), 1: (2,), 2: (3,), 3: (4,), -1: (-2,), -2: (-3,)},
    },
    "two": {
        2: {0: (1,)},
        4: {0: (1, -1, 2)},
        8: {0: (1, -1, 2, -2), 2: (3, 4), -2: (-3,)},
    },
    "direct": {
        2: {0: (1,)},
        4: {0: (1, -1, 2)},
        8: {0: (1, -1, 2, -2, 3, -3, 4)},
    },
}


def tree_of(kind, n, flip):
    sign = -1 if flip % 2 and n > 2 else 1
    return {sign * o: tuple(sign * t for t in to) for o, to in TREES[kind][n].items()}


def places_of(tree):
    found = [0]
    for o in found:
        found += tree.get(o, ())
    return found


def depth_of(tree, o):
    if o == 0:
        return 0
    return 1 + depth_of(tree, next(p for p, to in tree.items() if o in to))


def gather_plan(dims, kinds, flip):
    na, nb = SIZES[dims[0]], SIZES[dims[1]]
    ta = tree_of(kinds[0], na, flip)
    events = []
    for oa in places_of(ta):
        tb = tree_of(kinds[1], nb, oa + flip)
        for ob in places_of(tb):
            sends = []
            if ob == 0:
                sends += [(t, 0) for t in ta.get(oa, ())]
            sends += [(oa, t) for t in tb.get(ob, ())]
            cost = 3 * (depth_of(ta, oa) + depth_of(tb, ob)) + abs(oa) + abs(ob)
            events.append((cost, oa, ob, sends))
    return sorted(events, key=lambda e: e[0])


def partners(dims, kinds):
    found = {}
    for dim, kind in zip(dims, kinds):
        steps = found.setdefault(dim, set())
        for o, to in TREES[kind][SIZES[dim]].items():
            for t in to:
                steps |= {(t - o) % SIZES[dim], (o - t) % SIZES[dim]}
    return found


def greet(me, steps):
    barrier = pltpu.get_barrier_semaphore()
    count = 0
    for dim in sorted(steps):
        for step in sorted(steps[dim]):
            pl.semaphore_signal(
                barrier,
                inc=1,
                device_id=device_at(shifted(me, dim, step)),
                device_id_type=pl.DeviceIdType.MESH,
            )
            count += 1
    return lambda: pl.semaphore_wait(barrier, count)


def remote(source, place, send_sem, recv_sem, there):
    return pltpu.make_async_remote_copy(
        src_ref=source,
        dst_ref=place,
        send_sem=send_sem,
        recv_sem=recv_sem,
        device_id=device_at(there),
        device_id_type=pl.DeviceIdType.MESH,
    )


class Gather:
    def __init__(self, me, source, place, dims, kinds, flip, sems, base):
        self.me, self.source, self.place = me, source, place
        self.dims, self.kinds, self.flip = dims, kinds, flip
        self.send_sem, self.recv_sem, self.own_sem = sems
        self.plan = gather_plan(dims, kinds, flip)
        self.slots = {(oa, ob): base + k for k, (_, oa, ob, _) in enumerate(self.plan)}
        self.copies = []

    def at(self, oa, ob):
        origin = shifted(shifted(self.me, self.dims[0], -oa), self.dims[1], -ob)
        return self.place(index_in(origin, self.dims))

    def step(self, event):
        _, oa, ob, sends = event
        place = self.at(oa, ob)
        source = place
        if (oa, ob) == (0, 0):
            source = self.source
        else:
            slot = self.slots[oa, ob]
            near = shifted(self.me, self.dims[0], 1)
            remote(place, place, self.send_sem.at[0], self.recv_sem.at[slot], near).wait_recv()
        for to in sends:
            there = shifted(shifted(self.me, self.dims[0], to[0] - oa), self.dims[1], to[1] - ob)
            slot = self.slots[to]
            copy = remote(source, place, self.send_sem.at[slot], self.recv_sem.at[slot], there)
            copy.start()
            self.copies.append(copy)
        if (oa, ob) == (0, 0):
            self.own = pltpu.make_async_copy(source, place, self.own_sem)
            self.own.start()

    def finish(self):
        for copy in self.copies:
            copy.wait_send()


def run(*gathers):
    todo = [(e[0], n, e) for n, g in enumerate(gathers) for e in g.plan]
    for _, n, event in sorted(todo, key=lambda e: e[:2]):
        gathers[n].step(event)
    for g in gathers:
        g.own.wait()


def dot_f32(a, b):
    return jnp.dot(a, b, preferred_element_type=jnp.float32)


def split_three(x):
    high = x.astype(jnp.bfloat16)
    rest = x - high.astype(jnp.float32)
    middle = rest.astype(jnp.bfloat16)
    low = (rest - middle.astype(jnp.float32)).astype(jnp.bfloat16)
    return high, middle, low


def attend(scalars, q_ref, new_ref, cache_ref, left_ref, right_ref, queries, scores, weights):
    lengths, factor = scalars
    rows = q_ref.shape[0]
    scale = HEAD ** (-0.5)
    queries[...] = jnp.zeros_like(queries)
    for g in range(GROUP):
        queries[:, g, :] = q_ref[:, g * HEAD : (g + 1) * HEAD].astype(jnp.float32)
    lane = lax.broadcasted_iota(jnp.int32, (8, CACHE), 1)

    def along(j, r):
        row = jnp.full((8, CACHE), factor(j, 3, r))
        for b in (2, 1, 0):
            row = jnp.where(lane < (b + 1) * BLOCK_LEN, factor(j, b, r), row)
        return row

    for r in range(rows):
        raw = lax.dot_general(
            queries[r].astype(jnp.bfloat16),
            cache_ref[r, 0],
            (((1,), (1,)), ((), ())),
            preferred_element_type=jnp.float32,
        )
        scores[r] = jnp.where(lane < lengths[r], raw * along(0, r) * scale, -jnp.inf)
        weights[r] = along(1, r)
    fresh = new_ref[...].astype(jnp.float32)
    own = jnp.sum(queries[...] * fresh[:, 0:1, :], axis=2, keepdims=True) * scale
    s = scores[...]
    top = jnp.maximum(jnp.max(s, axis=2, keepdims=True), own)
    s = jnp.exp(s - top)
    own = jnp.exp(own - top)
    total = jnp.sum(s, axis=2, keepdims=True) + own
    weights[...] = s / total * weights[...]
    own = (own / total).astype(jnp.bfloat16).astype(jnp.float32) * fresh[:, 1:2, :]
    for r in range(rows):
        scores[r] = dot_f32(weights[r].astype(jnp.bfloat16), cache_ref[r, 1])
    scores[...] = scores[...] + own
    for g in range(GROUP):
        ref = left_ref if g < GROUP // 2 else right_ref
        at = g % (GROUP // 2)
        ref[:, at * HEAD : (at + 1) * HEAD] = scores[:, g, :].astype(ref.dtype)


def hand_off(cache_ref, factor, request, blocks, going_ref):
    for j in range(2):
        for b in range(CACHE // BLOCK_LEN):
            span = pl.ds(b * BLOCK_LEN, BLOCK_LEN)
            levels = cache_ref[request, j, span, :].astype(jnp.float32)
            going_ref[j, span, :] = jnp.where(
                b < blocks, levels * factor(j, b, request), 0.0
            ).astype(going_ref.dtype)


def route(choice_ref, slot_ref, pick_ref, expert):
    tokens = choice_ref.shape[1]
    experts = slot_ref.shape[0]
    ids = lax.broadcasted_iota(jnp.int32, (experts, tokens), 0)
    order = lax.broadcasted_iota(jnp.int32, (experts, tokens), 1)
    named = (choice_ref[0:1, :] == ids) | (choice_ref[1:2, :] == ids)
    count = named.astype(jnp.int32)
    step = 1
    while step < tokens:
        count = count + jnp.where(order >= step, pltpu.roll(count, step, 1), 0)
        step *= 2
    slots = jnp.where(named, count - 1, -1)
    slot_ref[...] = slots
    mine = jnp.sum(jnp.where(ids == expert, slots, 0).astype(jnp.float32).T, axis=1, keepdims=True)
    capacity = pick_ref.shape[1]
    across = lax.broadcasted_iota(jnp.int32, (tokens, capacity), 1).astype(jnp.float32)
    pick_ref[...] = (mine == across).astype(jnp.float32).astype(pick_ref.dtype)


def front_items():
    zy, yz, xc = ("z", "y"), ("y", "z"), ("x", "c")
    two, ring = ("two", "two"), ("ring", "ring")
    return {
        "left": (zy, two, 0),
        "right": (yz, two, 1),
        "part0": (xc, ring, 0),
        "part1": (xc, ring, 1),
        "going0": (zy, ring, 0),
        "going1": (yz, ring, 1),
        "rows0": (zy, ring, 0),
        "rows1": (yz, ring, 1),
        "extra": (yz, ring, 0),
    }


def members(item):
    return SIZES[item[0][0]] * SIZES[item[0][1]]


def front_body(*refs):
    hbm, outs, scratch = refs[:13], refs[13:18], refs[18:]
    u_ref, extra_ref, hidden_ref, came_ref, slot_ref = outs
    local_refs, scratch = scratch[:13], scratch[13:]
    (
        lengths,
        precision,
        scales,
        mig_req,
        mig_blocks,
        q_ref,
        new_ref,
        cache_ref,
        choice_ref,
        w_ref,
        stream_ref,
        gain_ref,
        router_ref,
    ) = local_refs
    (
        left_ref,
        right_ref,
        going_ref,
        pick_ref,
        queries,
        scores,
        weights,
        left_all,
        right_all,
        part_own,
        part_all,
        rows_own,
        extra_own,
        send_sem,
        recv_sem,
        own_sem,
        load_sem,
    ) = scratch
    me = coords()
    items = front_items()
    greeted = {}
    for dims, kinds, _ in items.values():
        for dim, steps in partners(dims, kinds).items():
            greeted.setdefault(dim, set()).update(steps)
    entered = greet(me, greeted)
    loads = [
        pltpu.make_async_copy(a, b, load_sem.at[k])
        for k, (a, b) in enumerate(zip(hbm, local_refs))
    ]
    for load in loads:
        load.start()

    def factor(j, b, r):
        return jnp.where(precision[b, r] == 1, scales[4 * j + b, r], 1.0)

    for load in loads[:8]:
        load.wait()
    attend(
        (lengths, factor), q_ref, new_ref, cache_ref, left_ref, right_ref, queries, scores, weights
    )
    rep = lax.axis_index("rep")
    entered()
    refs = {
        "left": (left_ref, lambda i: left_all.at[i]),
        "right": (right_ref, lambda i: right_all.at[i]),
        "part0": (part_own.at[0], lambda i: part_all.at[i, 0]),
        "part1": (part_own.at[1], lambda i: part_all.at[i, 1]),
        "going0": (going_ref.at[0], lambda i: came_ref.at[i, 0]),
        "going1": (going_ref.at[1], lambda i: came_ref.at[i, 1]),
        "rows0": (rows_own.at[0], lambda i: u_ref.at[i, 0]),
        "rows1": (rows_own.at[1], lambda i: u_ref.at[i, 1]),
        "extra": (extra_own, lambda i: extra_ref.at[i]),
    }
    g, base = {}, 0
    for n, (name, (dims, kinds, flip)) in enumerate(items.items()):
        sems = (send_sem, recv_sem, own_sem.at[n])
        g[name] = Gather(me, *refs[name], dims, kinds, flip, sems, base)
        base += members(items[name])
    moving = sorted(
        [(e[0], n, e) for n in (0, 1) for e in g["going%d" % n].plan], key=lambda e: e[:2]
    )

    def move(depth):
        while moving and moving[0][0] <= depth:
            _, n, event = moving.pop(0)
            g["going%d" % n].step(event)

    todo = sorted(
        [(e[0], n, e) for n, k in enumerate(("left", "right")) for e in g[k].plan],
        key=lambda e: e[:2],
    )
    for k, (cost, n, event) in enumerate(todo):
        if k == 2:
            hand_off(cache_ref, factor, mig_req[rep], mig_blocks[rep], going_ref)
            move(0)
            for load in loads[8:]:
                load.wait()
            route(choice_ref, slot_ref, pick_ref, lax.axis_index("hx"))
        g[("left", "right")[n]].step(event)
    for k in ("left", "right"):
        g[k].own.wait()

    split = left_ref.shape[1]
    tokens = stream_ref.shape[1]
    transposed = (((1,), (1,)), ((), ()))
    part = lax.dot_general(
        w_ref[:, :split],
        left_all[...].reshape(tokens, split),
        transposed,
        preferred_element_type=jnp.float32,
    ) + lax.dot_general(
        w_ref[:, split:],
        right_all[...].reshape(tokens, split),
        transposed,
        preferred_element_type=jnp.float32,
    )
    half = part_own.shape[1]
    for n in range(2):
        part_own[n] = part[n * half : (n + 1) * half].astype(part_own.dtype)
    todo = sorted(
        [(e[0], n, e) for n in range(2) for e in g["part%d" % n].plan], key=lambda e: e[:2]
    )
    for k, (cost, n, event) in enumerate(todo):
        if k == 2:
            move(4)
        if k == 6:
            move(8)
        g["part%d" % n].step(event)
    for k in ("part0", "part1"):
        g[k].own.wait()

    gain = jnp.broadcast_to(gain_ref[...], (8, gain_ref.shape[1])).T[:, :1]
    squares = jnp.zeros((1, tokens), jnp.float32)
    logits = jnp.zeros((router_ref.shape[0], tokens), jnp.float32)
    for n in range(2):
        span = pl.ds(n * half, half)
        hidden = stream_ref[span, :].astype(jnp.float32)
        for e in range(part_all.shape[0]):
            hidden = hidden + part_all[e, n].astype(jnp.float32)
        hidden_ref[span, :] = hidden
        gained = hidden * gain[n * half : (n + 1) * half]
        rows_own[n] = dot_f32(gained.astype(jnp.bfloat16), pick_ref[...]).astype(rows_own.dtype)
        g["rows%d" % n].step(g["rows%d" % n].plan.pop(0))
        squares = squares + jnp.sum(hidden * hidden, axis=0, keepdims=True)
        logits = logits + jnp.dot(
            router_ref[:, n * half : (n + 1) * half].astype(jnp.float32),
            gained,
            precision=lax.Precision.HIGHEST,
            preferred_element_type=jnp.float32,
        )
    ids = lax.broadcasted_iota(jnp.int32, logits.shape, 0)
    choice = choice_ref[...]
    first = jnp.sum(jnp.where(choice[0:1] == ids, logits, 0.0), axis=0, keepdims=True)
    second = jnp.sum(jnp.where(choice[1:2] == ids, logits, 0.0), axis=0, keepdims=True)
    ahead = jnp.where(choice[0:1] == lax.axis_index("hx"), first - second, second - first)
    terms = jnp.concatenate(
        [t.astype(jnp.float32) for t in split_three(squares) + split_three(ahead)]
        + [jnp.zeros((2, tokens), jnp.float32)],
        axis=0,
    ).astype(jnp.bfloat16)
    chosen = dot_f32(terms, pick_ref[...])
    extra_own[...] = jnp.concatenate(
        [
            chosen[0:1] + chosen[1:2] + chosen[2:3],
            chosen[3:4] + chosen[4:5] + chosen[5:6],
            chosen[2:8] * 0.0,
        ],
        axis=0,
    )
    move(11)
    todo = sorted(
        [(e[0], n, e) for n, k in enumerate(("rows0", "rows1", "extra")) for e in g[k].plan],
        key=lambda e: e[:2],
    )
    for cost, n, event in todo:
        if cost > 4:
            move(cost + 8)
        g[("rows0", "rows1", "extra")[n]].step(event)
    move(10**6)
    for k in ("rows0", "rows1", "extra", "going0", "going1"):
        g[k].own.wait()
    for k in g:
        g[k].finish()


def front(inputs, capacity, collective_id):
    query, stream = inputs[5], inputs[10]
    rows, wide = query.shape
    split = wide // 2
    mine, tokens = stream.shape
    half = mine // 2
    kind = query.dtype
    going = inputs[7].shape[1:]
    vmem = pl.BlockSpec(memory_space=pltpu.VMEM)
    anywhere = pl.BlockSpec(memory_space=pl.ANY)
    items = front_items()
    total = sum(members(item) for item in items.values())
    spaces = [pltpu.SMEM] * 5 + [pltpu.VMEM] * 8
    return pl.pallas_call(
        front_body,
        out_shape=[
            jax.ShapeDtypeStruct((32, 2, half, capacity), kind),
            jax.ShapeDtypeStruct((32, 8, capacity), jnp.float32),
            jax.ShapeDtypeStruct((mine, tokens), jnp.float32),
            jax.ShapeDtypeStruct((32, *going), kind),
            jax.ShapeDtypeStruct((8, tokens), jnp.int32),
        ],
        in_specs=[pl.BlockSpec(memory_space=pltpu.HBM)] * 13,
        out_specs=[anywhere, anywhere, vmem, anywhere, vmem],
        scratch_shapes=[space(x.shape, x.dtype) for space, x in zip(spaces, inputs)]
        + [
            pltpu.VMEM((rows, split), kind),
            pltpu.VMEM((rows, split), kind),
            pltpu.VMEM(going, kind),
            pltpu.VMEM((tokens, capacity), kind),
            pltpu.VMEM((rows, 8, HEAD), jnp.float32),
            pltpu.VMEM((rows, 8, HEAD), jnp.float32),
            pltpu.VMEM((rows, 8, HEAD), jnp.float32),
            pltpu.VMEM((32, rows, split), kind),
            pltpu.VMEM((32, rows, split), kind),
            pltpu.VMEM((2, half, tokens), kind),
            pltpu.VMEM((8, 2, half, tokens), kind),
            pltpu.VMEM((2, half, capacity), kind),
            pltpu.VMEM((8, capacity), jnp.float32),
            pltpu.SemaphoreType.DMA((total,)),
            pltpu.SemaphoreType.DMA((total,)),
            pltpu.SemaphoreType.DMA((len(items),)),
            pltpu.SemaphoreType.DMA((13,)),
        ],
        compiler_params=pltpu.CompilerParams(
            collective_id=collective_id, has_side_effects=True, vmem_limit_bytes=40 * 2**20
        ),
        name="front",
    )(*inputs)


def down_body(
    act_ref,
    w_hbm,
    gate_ref,
    hidden_hbm,
    slot_ref,
    came_hbm,
    dest_hbm,
    o_ref,
    arrived_ref,
    w_ref,
    hidden_ref,
    came_ref,
    dest_ref,
    p2,
    p1,
    pm,
    r1,
    fin,
    turned,
    tf,
    zr,
    place,
    out_own,
    out_all,
    *sems,
):
    s1_send, s1_recv, s2_send, s2_recv, z_send, z_recv, x_send, x_recv, x_own, load_sem = sems
    me = coords()
    xc, kinds = ("x", "c"), ("ring", "ring")
    entered = greet(me, {"y": {1, 3}, "z": set(range(1, 8)), **partners(xc, kinds)})
    group = w_ref.shape[1] // 4
    loads = {}
    for k, step in enumerate((2, 1, 3, 0)):
        start = pl.multiple_of(lax.rem(me["y"] + step, 4) * group, 128)
        span = pl.ds(start, group)
        loads[step] = pltpu.make_async_copy(w_hbm.at[:, span], w_ref.at[:, span], load_sem.at[k])
        loads[step].start()
    late = [
        pltpu.make_async_copy(a, b, load_sem.at[4 + k])
        for k, (a, b) in enumerate(
            ((hidden_hbm, hidden_ref), (came_hbm, came_ref), (dest_hbm, dest_ref))
        )
    ]
    up, down = shifted(me, "y", 1), shifted(me, "y", -1)
    pair, odd = me["z"] // 2, lax.rem(me["z"], 2)
    rows = act_ref.shape[0]
    mid = rows // 2
    wide = w_ref.shape[1] // 16
    low, high = pl.ds(0, mid), pl.ds(mid, mid)
    order = (2, 1, 3, 0)

    def product(step, k):
        there = lax.rem(me["y"] + step, 4)
        start = there * (4 * wide) + lax.rem(pair + k, 4) * wide
        return dot_f32(act_ref[...], w_ref[:, pl.ds(pl.multiple_of(start, 128), wide)])

    copies = []

    def send(source, place, ss, rs, there):
        copy = remote(source, place, ss, rs, there)
        copy.start()
        copies.append(copy)
        return copy

    steps = {}
    loads[2].wait()
    for k in order:
        p2[k] = product(2, k).astype(p2.dtype)
        if k == order[0]:
            entered()
        a = send(p2.at[k, low], r1.at[k, 0], s1_send.at[k, 0], s1_recv.at[k, 0], up)
        b = send(p2.at[k, high], r1.at[k, 1], s1_send.at[k, 1], s1_recv.at[k, 1], down)
        steps[k] = (a, b)
    tokens = slot_ref.shape[1]
    down_rows = lax.broadcasted_iota(jnp.int32, (rows, tokens), 0)

    def place_expert(e):
        place[e] = (slot_ref[e : e + 1, :] == down_rows).astype(jnp.float32).astype(place.dtype)

    lasts = {}
    loads[1].wait()
    loads[3].wait()
    for load in late:
        load.start()
    for k in order:
        p1[k] = product(1, k).astype(p1.dtype)
        c = send(p1.at[k, high], fin.at[k, 0, 1], s2_send.at[k, 0, 1], s2_recv.at[k, 0, 1], up)
        pm[k] = product(3, k).astype(pm.dtype)
        d = send(pm.at[k, low], fin.at[k, 1, 0], s2_send.at[k, 1, 0], s2_recv.at[k, 1, 0], down)
        steps[k][0].wait_recv()
        p1[k, low] = (p1[k, low].astype(jnp.float32) + r1[k, 0].astype(jnp.float32)).astype(p1.dtype)
        e = send(p1.at[k, low], fin.at[k, 0, 0], s2_send.at[k, 0, 0], s2_recv.at[k, 0, 0], up)
        steps[k][1].wait_recv()
        pm[k, high] = (pm[k, high].astype(jnp.float32) + r1[k, 1].astype(jnp.float32)).astype(
            pm.dtype
        )
        f = send(pm.at[k, high], fin.at[k, 1, 1], s2_send.at[k, 1, 1], s2_recv.at[k, 1, 1], down)
        lasts[k] = (c, d, e, f)
    loads[0].wait()
    for load in late:
        load.wait()
    rep = lax.axis_index("rep")
    n_rep = dest_ref.shape[0]
    first, last = jnp.int32(n_rep), jnp.int32(-1)
    for source in range(n_rep):
        aimed = dest_ref[source] == rep
        first = jnp.where(aimed, jnp.minimum(first, source), first)
        last = jnp.where(aimed, source, last)
    for q, (source, there) in enumerate(((first, last >= 0), (last, last > first))):
        block = came_ref[jnp.clip(source, 0, n_rep - 1)].astype(jnp.float32)
        arrived_ref[0, q] = jnp.where(there, block, 0.0).astype(arrived_ref.dtype)
    for k in order:
        whole = product(0, k)
        for copy in lasts[k]:
            copy.wait_recv()
        whole = whole + jnp.concatenate(
            [
                fin[k, 0, 0].astype(jnp.float32) + fin[k, 1, 0].astype(jnp.float32),
                fin[k, 0, 1].astype(jnp.float32) + fin[k, 1, 1].astype(jnp.float32),
            ],
            axis=0,
        )
        whole = whole.T
        for e in range(2):
            part = whole[e * (wide // 2) : (e + 1) * (wide // 2)]
            turned[k, e] = part.astype(turned.dtype)
            if k == 0:
                tf[e] = part
        first = 2 * lax.rem(pair + k, 4)
        for e in range(2):
            if k > 0:
                there = dict(me, z=first + e)
                send(
                    turned.at[k, e],
                    zr.at[2 * k + odd],
                    z_send.at[2 * k + e],
                    z_recv.at[2 * k + odd],
                    there,
                )
        if k == 0:
            there = dict(me, z=first + 1 - odd)
            send(turned.at[0, 1 - odd], zr.at[odd], z_send.at[0], z_recv.at[odd], there)
    total = tf[odd]
    for k in order:
        for e in range(2) if k > 0 else (0,):
            slot = 2 * k + e if k > 0 else 1 - odd
            remote(zr.at[slot], zr.at[slot], z_send.at[0], z_recv.at[slot], up).wait_recv()
            total = total + zr[slot].astype(jnp.float32)
    total = total * gate_ref[...]
    n = out_own.shape[1]
    across = []
    for h in range(2):
        out_own[h] = total[h * n : (h + 1) * n].astype(out_own.dtype)
        across.append(
            Gather(
                me,
                out_own.at[h],
                lambda i, h=h: out_all.at[i, h],
                xc,
                kinds,
                h,
                (x_send, x_recv, x_own.at[h]),
                8 * h,
            )
        )
    for gather in across:
        gather.step(gather.plan.pop(0))
    for e in range(8):
        place_expert(e)
    run(*across)
    for h in range(2):
        span = pl.ds(h * n, n)
        mixed = hidden_ref[span, :]
        for e in range(8):
            mixed = mixed + dot_f32(out_all[e, h], place[e])
        o_ref[span, :] = mixed.astype(o_ref.dtype)
    for copy in copies:
        copy.wait_send()
    for gather in across:
        gather.finish()


def down_and_scatter(act, w_down, gate, hidden, slots, came, mig_dest, collective_id):
    rows, depth = act.shape
    width = w_down.shape[1] // 16
    vmem = pl.BlockSpec(memory_space=pltpu.VMEM)
    hbm = pl.BlockSpec(memory_space=pltpu.HBM)
    kind = act.dtype
    return pl.pallas_call(
        down_body,
        out_shape=[
            jax.ShapeDtypeStruct(hidden.shape, kind),
            jax.ShapeDtypeStruct((1, IN_MOST, *came.shape[1:]), kind),
        ],
        in_specs=[vmem, hbm, vmem, hbm, vmem, hbm, hbm],
        out_specs=[vmem, vmem],
        scratch_shapes=[
            pltpu.VMEM(w_down.shape, kind),
            pltpu.VMEM(hidden.shape, hidden.dtype),
            pltpu.VMEM(came.shape, kind),
            pltpu.SMEM(mig_dest.shape, mig_dest.dtype),
            pltpu.VMEM((4, rows, width), kind),
            pltpu.VMEM((4, rows, width), kind),
            pltpu.VMEM((4, rows, width), kind),
            pltpu.VMEM((4, 2, rows // 2, width), kind),
            pltpu.VMEM((4, 2, 2, rows // 2, width), kind),
            pltpu.VMEM((4, 2, width // 2, rows), kind),
            pltpu.VMEM((2, width // 2, rows), jnp.float32),
            pltpu.VMEM((8, width // 2, rows), kind),
            pltpu.VMEM((8, rows, slots.shape[1]), kind),
            pltpu.VMEM((2, width // 4, rows), kind),
            pltpu.VMEM((8, 2, width // 4, rows), kind),
            pltpu.SemaphoreType.DMA((4, 2)),
            pltpu.SemaphoreType.DMA((4, 2)),
            pltpu.SemaphoreType.DMA((4, 2, 2)),
            pltpu.SemaphoreType.DMA((4, 2, 2)),
            pltpu.SemaphoreType.DMA((8,)),
            pltpu.SemaphoreType.DMA((8,)),
            pltpu.SemaphoreType.DMA((16,)),
            pltpu.SemaphoreType.DMA((16,)),
            pltpu.SemaphoreType.DMA((2,)),
            pltpu.SemaphoreType.DMA((7,)),
        ],
        compiler_params=pltpu.CompilerParams(
            collective_id=collective_id, has_side_effects=True, vmem_limit_bytes=56 * 2**20
        ),
        name="down_scatter",
    )(act, w_down, gate, hidden, slots, came, mig_dest)


def contract_first(a, b, **kw):
    return lax.dot_general(
        a, b, (((0,), (0,)), ((), ())), preferred_element_type=jnp.float32, **kw
    )


def local(
    stream_in,
    query,
    new_kv,
    cache,
    precision,
    cache_scale,
    lengths,
    w_heads,
    norm_gain,
    w_router,
    expert_choice,
    w_in,
    w_down,
    mig_dest,
    mig_req,
    mig_blocks,
):
    tokens = stream_in.shape[0]
    capacity = tokens // 2
    ff = w_in.shape[3]
    choice = expert_choice.T
    rows = query.shape[0]
    u_all, extra_all, hidden, came, slots = front(
        [
            lengths,
            precision.T,
            jnp.transpose(cache_scale[..., 0], (1, 2, 0)).reshape(-1, rows),
            mig_req,
            mig_blocks,
            query,
            new_kv,
            cache,
            choice,
            w_heads.T,
            stream_in.T,
            norm_gain[None],
            w_router.T,
        ],
        capacity,
        1,
    )
    sums = jnp.sum(extra_all, axis=0)
    inverse = lax.rsqrt(sums[0] / D + EPSILON)
    gate_of_slot = 1.0 / (1.0 + jnp.exp(-sums[1] * inverse))
    gate_up = contract_first(w_in[0].reshape(D, 2 * ff), u_all.reshape(D, capacity))
    gate_up = gate_up * inverse[None, :]
    act = (jax.nn.silu(gate_up[:ff]) * gate_up[ff:]).astype(jnp.bfloat16)
    mixed, arrived = down_and_scatter(
        act.T, w_down[0], gate_of_slot[None], hidden, slots, came, mig_dest, 2
    )
    return (mixed.T, arrived)


def solution(mesh):
    placed = (
        P(None, "rep"),
        P("rep", "hx"),
        P("rep", None, "hx"),
        P("rep", None, None, "hx"),
        P("rep", None),
        P("rep", None, None, "hx"),
        P("rep"),
        P("hx", "rep"),
        P("rep"),
        P("rep", None),
        P(),
        P("hx", None, None, "rep"),
        P("hx", "rep", None),
        P(),
        P(),
        P(),
    )
    return jax.shard_map(
        local,
        mesh=mesh,
        in_specs=placed,
        out_specs=(P(None, "rep"), P("rep", None, None, None, "hx")),
        check_vma=False,
    )
```

time: 206 us -> 178 us (0.86)
  other arithmetic: 11.4 us -> 1.45 us
  matrix products: 15.4 us -> 6.52 us
  between operations: 8.73 us -> 0.86 us
  Pallas kernels: 159 us -> 153 us
  local copies, waits for them, and re-layouts: 10.6 us -> 15 us
    dot_general x9 -> x0, matrix products: 12.4 us -> none  [the longest x1 4.04 us: local(): lax.dot_general(everyone.reshape(experts, mine, capacity), place, (((0, 2...]
    unnamed x23 -> x37, local copies, waits for them, and re-layouts: 5.46 us -> 15 us
    pallas_call x5 -> x2, Pallas kernels: 159 us -> 153 us  [the longest x1 85.4 us: front(): pl.pallas_call(front_body, out_shape=[jax.ShapeDtypeStruct((32, 2, half,...]
    dot_general x2 -> x1, matrix products: 3.04 us -> 6.52 us  [contract_first(): lax.dot_general(a, b, (((0,), (0,)), ((), ())), preferred_element_type=jn...]
    dynamic_slice x4 -> x0, local copies, waits for them, and re-layouts: 2.52 us -> none  [the longest x1 1.24 us: hand_off(): chosen_req = mig_req[replica_id]]
    reduce_sum x3 -> x0, other arithmetic: 2.35 us -> none  [the longest x1 2.05 us: local(): jnp.sum(parts.reshape(experts, mine, tokens).astype(jnp.float32), axis=0)]
    select_n x3 -> x0, other arithmetic: 2.21 us -> none  [the longest x1 1.51 us: arrivals(): rows.append(jnp.where(there, row, jnp.zeros((), row.dtype)))]
where the time goes in v3:
time: 178 us; the launch traced here: 177 us
  Pallas kernels  153 us (86%)
  local copies, waits for them, and re-layouts  15 us (8%)
  matrix products  6.52 us (4%)
    pallas_call x1, Pallas kernels, front(): pl.pallas_call(front_body, out_shape=[jax.ShapeDtypeStruct((32, 2, half,...  85.4 us
    pallas_call x1, Pallas kernels, down_and_scatter(): pl.pallas_call(down_body, out_shape=[jax.ShapeDtypeStruct(hidden.shape, k...  67.8 us
    unnamed x37, local copies, waits for them, and re-layouts  15 us
    dot_general x1, matrix products, contract_first(): lax.dot_general(a, b, (((0,), (0,)), ((), ())), preferred_element_type=jn...  6.52 us

profile of v3, /device:TPU:1, one launch (start us, length us, event | category | flops | bytes accessed | tf_op | source)
XLA Modules:
  0.0 177.0 jit_solution(258344867431222292)
XLA Ops:
  0.6 0.0 copy-start.2
  0.6 0.0 copy-start.4
  0.7 0.0 copy-start.5
  0.7 0.0 copy-start.6
  0.7 0.0 copy-start.8
  0.7 0.0 copy-start.9
  0.7 0.0 copy-start.10
  0.7 0.0 copy-start.11
  0.7 0.0 copy-start.12
  0.7 0.0 copy-start.13
  0.7 0.0 copy-start.14
  0.7 0.0 copy-start.15
  0.8 0.0 copy-start.16
  0.8 6.6 %copy.18 = bf16[768,8,2,256]{3,1,2,0:T(8,128)(2,1)} copy(bf16[768,8,2,256]{3,2,1,0:T(2,128)(2,1)} %bitcast.32) | data formatting | bytes 12582912
  7.4 0.0 copy-done.2
  7.4 0.0 copy-done.4
  7.4 0.0 copy-done.5
  7.4 0.0 copy-done.6
  7.4 0.0 copy-done.8
  7.4 0.0 copy-done.9
  7.4 0.0 copy-done.10
  7.4 0.0 copy-done.11
  7.4 0.0 copy-done.12
  7.4 0.0 copy-done.13
  7.5 0.0 copy-done.14
  7.5 0.0 copy-done.15
  7.5 0.0 copy-done.16
  7.5 85.4 %front.1 = (bf16[32,2,96,384]{3,2,1,0:T(8,128)(2,1)S(1)}, f32[32,8,384]{2,1,0:T(8,128)S(1)}, f32[192,768]{1,0:T(8,128)S(1)}, bf16[32,2,128,128]{3,2,1,0:T(8,128)(2,1)S(1)}, s32[8,768]{1,0:T(8,128)S(1)}) custom-call(s32[24]{0:T(128)S(1)} %copy-done.14, s32[4,24]{1,0:T(4,128)S(1)} %bitcast.29, f32[8,24]{1,0:T(8,128)S(1)} %bitcast.27, s32[32]{0:T(128)S(1)} %copy-done.15, ...), custom_call_target="tpu_custom_call" | custom-call | tf_op jit(solution)/shard_map/front/pallas_call | solution.py:482
  92.9 0.0 copy-start
  92.9 2.2 %copy-done = bf16[32,2,96,384]{3,2,1,0:T(8,128)(2,1)} copy-done((bf16[32,2,96,384]{3,2,1,0:T(8,128)(2,1)}, bf16[32,2,96,384]{3,2,1,0:T(8,128)(2,1)S(1)}, u32[]{:S(2)}) %copy-start) | copy-done | bytes 4718616
  95.1 0.0 copy-start.1
  95.1 1.4 copy-done.1
  96.5 0.0 copy-start.3
  96.6 0.8 copy-done.3
  97.4 0.0 copy-start.7
  97.4 0.6 copy-done.7
  98.0 0.6 add_divide_fusion
  98.6 6.5 %fusion = f32[512,384]{0,1:T(8,128)S(1)} fusion(bf16[6144,384]{1,0:T(8,128)(2,1)} %bitcast.23, bf16[6144,512]{1,0:T(8,128)(2,1)} %bitcast.31, f32[384]{0:T(512)S(1)} %get-tuple-element.17), kind=kOutput, calls=%fused_computation.1 | convolution fusion | flops 2416115712 | bytes 11798016 | tf_op jit(solution)/shard_map/dot_general | solution.py:752
  105.2 0.8 fusion.2.act_ref
  106.0 67.8 %down_scatter.1 = (bf16[192,768]{1,0:T(8,128)(2,1)}, bf16[1,2,2,128,128]{4,3,2,1,0:T(8,128)(2,1)}) custom-call(bf16[384,256]{1,0:T(8,128)(2,1)} %fusion.2.act_ref, bf16[256,6144]{1,0:T(8,128)(2,1)} %bitcast.33, f32[1,384]{1,0:T(1,128)} %get-tuple-element.16.gate_ref, f32[192,768]{1,0:T(8,128)} %copy-done.3, s32[8,768]{1,0:T(8,128)} %copy-done.7, ...), custom_call_target="tpu_custom_call" | custom-call | tf_op jit(solution)/shard_map/down_scatter/pallas_call | solution.py:709
  173.7 1.7 copy.21
  175.4 1.6 copy.22
  (1 shorter events, 0.0 us)
Async XLA Ops:
  0.6 6.7 %copy-start.2 = (bf16[24,2,128,128]{3,2,1,0:T(8,128)(2,1)S(1)}, bf16[24,2,128,128]{3,2,1,0:T(8,128)(2,1)}, u32[]{:S(2)}) copy-start(bf16[24,2,128,128]{3,2,1,0:T(8,128)(2,1)} %refs_7_.1) | copy-start | bytes 4718596
  0.6 6.7 %copy-start.4 = (bf16[768,192]{0,1:T(8,128)(2,1)S(1)}, bf16[768,192]{0,1:T(8,128)(2,1)}, u32[]{:S(2)}) copy-start(bf16[768,192]{0,1:T(8,128)(2,1)} %param.23) | copy-start | bytes 884740
  0.7 6.7 %copy-start.5 = (bf16[768,192]{0,1:T(8,128)(2,1)S(1)}, bf16[768,192]{0,1:T(8,128)(2,1)}, u32[]{:S(2)}) copy-start(bf16[768,192]{0,1:T(8,128)(2,1)} %param.16) | copy-start | bytes 884740
  0.7 6.7 %copy-start.6 = (bf16[24,768]{1,0:T(8,128)(2,1)S(1)}, bf16[24,768]{1,0:T(8,128)(2,1)}, u32[]{:S(2)}) copy-start(bf16[24,768]{1,0:T(8,128)(2,1)} %refs_5_.1) | copy-start | bytes 110596
  0.7 6.7 %copy-start.8 = (bf16[24,2,128]{2,1,0:T(2,128)(2,1)S(1)}, bf16[24,2,128]{2,1,0:T(2,128)(2,1)}, u32[]{:S(2)}) copy-start(bf16[24,2,128]{2,1,0:T(2,128)(2,1)} %refs_6_.1) | copy-start | bytes 36868
  0.7 6.7 %copy-start.9 = (s32[768,2]{0,1:T(2,128)S(1)}, s32[768,2]{0,1:T(2,128)}, u32[]{:S(2)}) copy-start(s32[768,2]{0,1:T(2,128)} %param.26) | copy-start | bytes 18436
  0.7 6.7 %copy-start.10 = (f32[24,2,4,1]{0,3,2,1:T(1,128)S(1)}, f32[24,2,4,1]{0,3,2,1:T(1,128)}, u32[]{:S(2)}) copy-start(f32[24,2,4,1]{0,3,2,1:T(1,128)} %param.21) | copy-start | bytes 2308
  0.7 6.7 %copy-start.11 = (bf16[192,8]{0,1:T(8,128)(2,1)S(1)}, bf16[192,8]{0,1:T(8,128)(2,1)}, u32[]{:S(2)}) copy-start(bf16[192,8]{0,1:T(8,128)(2,1)} %param.25) | copy-start | bytes 9220
  0.7 6.7 %copy-start.12 = (s32[24,4]{0,1:T(4,128)S(1)}, s32[24,4]{0,1:T(4,128)}, u32[]{:S(2)}) copy-start(s32[24,4]{0,1:T(4,128)} %param.20) | copy-start | bytes 1156
  0.7 6.7 %copy-start.13 = (f32[192]{0:T(256)S(1)}, f32[192]{0:T(256)}, u32[]{:S(2)}) copy-start(f32[192]{0:T(256)} %param.24) | copy-start | bytes 2308
  0.7 6.7 %copy-start.14 = (s32[24]{0:T(128)S(1)}, s32[24]{0:T(128)}, u32[]{:S(2)}) copy-start(s32[24]{0:T(128)} %refs_0_.1) | copy-start | bytes 292
  0.7 6.7 %copy-start.15 = (s32[32]{0:T(128)S(1)}, s32[32]{0:T(128)}, u32[]{:S(2)}) copy-start(s32[32]{0:T(128)} %refs_3_.1) | copy-start | bytes 388
  0.8 6.7 %copy-start.16 = (s32[32]{0:T(128)S(1)}, s32[32]{0:T(128)}, u32[]{:S(2)}) copy-start(s32[32]{0:T(128)} %refs_4_.1) | copy-start | bytes 388
  92.9 2.2 %copy-start = (bf16[32,2,96,384]{3,2,1,0:T(8,128)(2,1)}, bf16[32,2,96,384]{3,2,1,0:T(8,128)(2,1)S(1)}, u32[]{:S(2)}) copy-start(bf16[32,2,96,384]{3,2,1,0:T(8,128)(2,1)S(1)} %get-tuple-element.9) | copy-start | bytes 14155780
  95.1 1.4 copy-start.1
  96.5 0.8 copy-start.3
  97.4 0.6 copy-start.7

commit v4 on v3

--- a/solution.py
+++ b/solution.py
@@ -267,14 +267,16 @@
     return {
         "left": (zy, two, 0),
         "right": (yz, two, 1),
-        "part0": (xc, ring, 0),
-        "part1": (xc, ring, 1),
+        **{"part%d" % n: (xc, ring, n) for n in range(4)},
         "going0": (zy, ring, 0),
         "going1": (yz, ring, 1),
-        "rows0": (zy, ring, 0),
-        "rows1": (yz, ring, 1),
+        **{"rows%d" % n: (zy if n % 2 == 0 else yz, ring, n // 2 + n % 2) for n in range(4)},
         "extra": (yz, ring, 0),
     }
+
+
+PIECES = ((0, 64), (64, 32), (96, 48), (144, 48))
+PARTS = ((0, 48), (48, 48), (96, 48), (144, 48))
 
 
 def members(item):
@@ -346,12 +348,22 @@
     refs = {
         "left": (left_ref, lambda i: left_all.at[i]),
         "right": (right_ref, lambda i: right_all.at[i]),
-        "part0": (part_own.at[0], lambda i: part_all.at[i, 0]),
-        "part1": (part_own.at[1], lambda i: part_all.at[i, 1]),
+        **{
+            "part%d" % n: (
+                part_own.at[pl.ds(*piece)],
+                lambda i, piece=piece: part_all.at[i, pl.ds(*piece)],
+            )
+            for n, piece in enumerate(PARTS)
+        },
         "going0": (going_ref.at[0], lambda i: came_ref.at[i, 0]),
         "going1": (going_ref.at[1], lambda i: came_ref.at[i, 1]),
-        "rows0": (rows_own.at[0], lambda i: u_ref.at[i, 0]),
-        "rows1": (rows_own.at[1], lambda i: u_ref.at[i, 1]),
+        **{
+            "rows%d" % n: (
+                rows_own.at[pl.ds(*piece)],
+                lambda i, piece=piece: u_ref.at[i, pl.ds(*piece)],
+            )
+            for n, piece in enumerate(PIECES)
+        },
         "extra": (extra_own, lambda i: extra_ref.at[i]),
     }
     g, base = {}, 0
@@ -386,44 +398,50 @@
     split = left_ref.shape[1]
     tokens = stream_ref.shape[1]
     transposed = (((1,), (1,)), ((), ()))
-    part = lax.dot_general(
-        w_ref[:, :split],
-        left_all[...].reshape(tokens, split),
-        transposed,
-        preferred_element_type=jnp.float32,
-    ) + lax.dot_general(
-        w_ref[:, split:],
-        right_all[...].reshape(tokens, split),
-        transposed,
-        preferred_element_type=jnp.float32,
-    )
-    half = part_own.shape[1]
+    half = stream_ref.shape[0] // 2
     for n in range(2):
-        part_own[n] = part[n * half : (n + 1) * half].astype(part_own.dtype)
-    todo = sorted(
-        [(e[0], n, e) for n in range(2) for e in g["part%d" % n].plan], key=lambda e: e[:2]
-    )
-    for k, (cost, n, event) in enumerate(todo):
-        if k == 2:
-            move(4)
-        if k == 6:
-            move(8)
-        g["part%d" % n].step(event)
-    for k in ("part0", "part1"):
-        g[k].own.wait()
+        span = pl.ds(n * half, half)
+        part = lax.dot_general(
+            w_ref[span, :split],
+            left_all[...].reshape(tokens, split),
+            transposed,
+            preferred_element_type=jnp.float32,
+        ) + lax.dot_general(
+            w_ref[span, split:],
+            right_all[...].reshape(tokens, split),
+            transposed,
+            preferred_element_type=jnp.float32,
+        )
+        part_own[span, :] = part.astype(part_own.dtype)
+        for k in (2 * n, 2 * n + 1):
+            g["part%d" % k].step(g["part%d" % k].plan.pop(0))
+    move(4)
+
+    def early(n):
+        names = ["part%d" % k for k in (2 * n, 2 * n + 1)]
+        found = sorted([(e[0], k, e) for k in names for e in g[k].plan], key=lambda e: e[:2])
+        for _, k, event in found:
+            g[k].step(event)
+        for k in names:
+            g[k].own.wait()
+        move(8)
 
     gain = jnp.broadcast_to(gain_ref[...], (8, gain_ref.shape[1])).T[:, :1]
     squares = jnp.zeros((1, tokens), jnp.float32)
     logits = jnp.zeros((router_ref.shape[0], tokens), jnp.float32)
     for n in range(2):
         span = pl.ds(n * half, half)
+        early(n)
         hidden = stream_ref[span, :].astype(jnp.float32)
         for e in range(part_all.shape[0]):
-            hidden = hidden + part_all[e, n].astype(jnp.float32)
+            hidden = hidden + part_all[e, span, :].astype(jnp.float32)
         hidden_ref[span, :] = hidden
         gained = hidden * gain[n * half : (n + 1) * half]
-        rows_own[n] = dot_f32(gained.astype(jnp.bfloat16), pick_ref[...]).astype(rows_own.dtype)
-        g["rows%d" % n].step(g["rows%d" % n].plan.pop(0))
+        rows_own[span, :] = dot_f32(gained.astype(jnp.bfloat16), pick_ref[...]).astype(
+            rows_own.dtype
+        )
+        for k in (2 * n, 2 * n + 1):
+            g["rows%d" % k].step(g["rows%d" % k].plan.pop(0))
         squares = squares + jnp.sum(hidden * hidden, axis=0, keepdims=True)
         logits = logits + jnp.dot(
             router_ref[:, n * half : (n + 1) * half].astype(jnp.float32),
@@ -451,16 +469,17 @@
         axis=0,
     )
     move(11)
+    last = ("rows0", "rows1", "rows2", "rows3", "extra")
     todo = sorted(
-        [(e[0], n, e) for n, k in enumerate(("rows0", "rows1", "extra")) for e in g[k].plan],
+        [(e[0], n, e) for n, k in enumerate(last) for e in g[k].plan],
         key=lambda e: e[:2],
     )
     for cost, n, event in todo:
-        if cost > 4:
-            move(cost + 8)
-        g[("rows0", "rows1", "extra")[n]].step(event)
+        if cost > 8:
+            move(cost + 2)
+        g[last[n]].step(event)
     move(10**6)
-    for k in ("rows0", "rows1", "extra", "going0", "going1"):
+    for k in (*last, "going0", "going1"):
         g[k].own.wait()
     for k in g:
         g[k].finish()
@@ -482,7 +501,7 @@
     return pl.pallas_call(
         front_body,
         out_shape=[
-            jax.ShapeDtypeStruct((32, 2, half, capacity), kind),
+            jax.ShapeDtypeStruct((32, mine, capacity), kind),
             jax.ShapeDtypeStruct((32, 8, capacity), jnp.float32),
             jax.ShapeDtypeStruct((mine, tokens), jnp.float32),
             jax.ShapeDtypeStruct((32, *going), kind),
@@ -501,9 +520,9 @@
             pltpu.VMEM((rows, 8, HEAD), jnp.float32),
             pltpu.VMEM((32, rows, split), kind),
             pltpu.VMEM((32, rows, split), kind),
-            pltpu.VMEM((2, half, tokens), kind),
-            pltpu.VMEM((8, 2, half, tokens), kind),
-            pltpu.VMEM((2, half, capacity), kind),
+            pltpu.VMEM((mine, tokens), kind),
+            pltpu.VMEM((8, mine, tokens), kind),
+            pltpu.VMEM((mine, capacity), kind),
             pltpu.VMEM((8, capacity), jnp.float32),
             pltpu.SemaphoreType.DMA((total,)),
             pltpu.SemaphoreType.DMA((total,)),
@@ -511,10 +530,13 @@
             pltpu.SemaphoreType.DMA((13,)),
         ],
         compiler_params=pltpu.CompilerParams(
-            collective_id=collective_id, has_side_effects=True, vmem_limit_bytes=40 * 2**20
+            collective_id=collective_id, has_side_effects=True, vmem_limit_bytes=62 * 2**20
         ),
         name="front",
     )(*inputs)
+
+
+SPANS = ((0, 256), (256, 128))
 
 
 def down_body(
@@ -536,15 +558,11 @@
     pm,
     r1,
     fin,
-    turned,
-    tf,
-    zr,
     place,
-    out_own,
-    out_all,
-    *sems,
+    *rest,
 ):
-    s1_send, s1_recv, s2_send, s2_recv, z_send, z_recv, x_send, x_recv, x_own, load_sem = sems
+    s1_send, s1_recv, s2_send, s2_recv, z_send, z_recv, x_send, x_recv, x_own, load_sem = rest[10:]
+    turned, tf, zr, out_own, out_all = (rest[2 * k : 2 * k + 2] for k in range(5))
     me = coords()
     xc, kinds = ("x", "c"), ("ring", "ring")
     entered = greet(me, {"y": {1, 3}, "z": set(range(1, 8)), **partners(xc, kinds)})
@@ -563,18 +581,17 @@
     ]
     up, down = shifted(me, "y", 1), shifted(me, "y", -1)
     pair, odd = me["z"] // 2, lax.rem(me["z"], 2)
-    rows = act_ref.shape[0]
-    mid = rows // 2
     wide = w_ref.shape[1] // 16
-    low, high = pl.ds(0, mid), pl.ds(mid, mid)
+    n = wide // 4
     order = (2, 1, 3, 0)
-
-    def product(step, k):
+    tokens = slot_ref.shape[1]
+    copies, firsts, lasts, across = [], {}, {}, {}
+
+    def product(p, step, k):
         there = lax.rem(me["y"] + step, 4)
         start = there * (4 * wide) + lax.rem(pair + k, 4) * wide
-        return dot_f32(act_ref[...], w_ref[:, pl.ds(pl.multiple_of(start, 128), wide)])
-
-    copies = []
+        rows = act_ref[pl.ds(*SPANS[p]), :]
+        return dot_f32(rows, w_ref[:, pl.ds(pl.multiple_of(start, 128), wide)])
 
     def send(source, place, ss, rs, there):
         copy = remote(source, place, ss, rs, there)
@@ -582,41 +599,139 @@
         copies.append(copy)
         return copy
 
-    steps = {}
+    def halves(p):
+        first, size = SPANS[p]
+        return pl.ds(first, size // 2), pl.ds(first + size // 2, size // 2)
+
+    def begin(p, k):
+        low, high = halves(p)
+        p2[k, pl.ds(*SPANS[p])] = product(p, 2, k).astype(p2.dtype)
+        if (p, k) == (0, order[0]):
+            entered()
+        firsts[p, k] = (
+            send(p2.at[k, low], r1.at[k, low], s1_send.at[p, k, 0], s1_recv.at[p, k, 0], up),
+            send(p2.at[k, high], r1.at[k, high], s1_send.at[p, k, 1], s1_recv.at[p, k, 1], down),
+        )
+
+    def middle(p, k):
+        low, high = halves(p)
+
+        def on(source, side, piece, there):
+            at = (p, k, side, 0 if piece is low else 1)
+            return send(
+                source.at[k, piece], fin.at[k, side, piece], s2_send.at[at], s2_recv.at[at], there
+            )
+
+        p1[k, pl.ds(*SPANS[p])] = product(p, 1, k).astype(p1.dtype)
+        c = on(p1, 0, high, up)
+        pm[k, pl.ds(*SPANS[p])] = product(p, 3, k).astype(pm.dtype)
+        d = on(pm, 1, low, down)
+        firsts[p, k][0].wait_recv()
+        p1[k, low] = (p1[k, low].astype(jnp.float32) + r1[k, low].astype(jnp.float32)).astype(
+            p1.dtype
+        )
+        e = on(p1, 0, low, up)
+        firsts[p, k][1].wait_recv()
+        pm[k, high] = (pm[k, high].astype(jnp.float32) + r1[k, high].astype(jnp.float32)).astype(
+            pm.dtype
+        )
+        lasts[p, k] = (c, d, e, on(pm, 1, high, down))
+
+    def end(p, k):
+        whole = product(p, 0, k)
+        for copy in lasts[p, k]:
+            copy.wait_recv()
+        span = pl.ds(*SPANS[p])
+        whole = whole + (fin[k, 0, span].astype(jnp.float32) + fin[k, 1, span].astype(jnp.float32))
+        whole = whole.T
+        for e in range(2):
+            part = whole[e * (wide // 2) : (e + 1) * (wide // 2)]
+            turned[p][k, e] = part.astype(turned[p].dtype)
+            if k == 0:
+                tf[p][e] = part
+        first = 2 * lax.rem(pair + k, 4)
+        if k > 0:
+            for e in range(2):
+                slot = 2 * k + odd
+                send(
+                    turned[p].at[k, e],
+                    zr[p].at[slot],
+                    z_send.at[p, 2 * k + e],
+                    z_recv.at[p, slot],
+                    dict(me, z=first + e),
+                )
+        else:
+            send(
+                turned[p].at[0, 1 - odd],
+                zr[p].at[odd],
+                z_send.at[p, 0],
+                z_recv.at[p, odd],
+                dict(me, z=first + 1 - odd),
+            )
+
+    def total(p):
+        found = tf[p][odd]
+        for k in order:
+            for e in range(2) if k > 0 else (0,):
+                slot = 2 * k + e if k > 0 else 1 - odd
+                remote(
+                    zr[p].at[slot], zr[p].at[slot], z_send.at[p, 0], z_recv.at[p, slot], up
+                ).wait_recv()
+                found = found + zr[p][slot].astype(jnp.float32)
+        found = found * gate_ref[:, pl.ds(*SPANS[p])]
+        for h in range(2):
+            out_own[p][h] = found[h * n : (h + 1) * n].astype(out_own[p].dtype)
+            gather = Gather(
+                me,
+                out_own[p].at[h],
+                lambda i, h=h: out_all[p].at[i, h],
+                xc,
+                kinds,
+                h,
+                (x_send, x_recv, x_own.at[2 * p + h]),
+                8 * (2 * p + h),
+            )
+            gather.step(gather.plan.pop(0))
+            across[p, h] = gather
+
+    def one_hot(p):
+        first, size = SPANS[p]
+        slots = lax.broadcasted_iota(jnp.int32, (size, tokens), 0) + first
+        for e in range(8):
+            place[e, pl.ds(first, size)] = (
+                (slot_ref[e : e + 1, :] == slots).astype(jnp.float32).astype(place.dtype)
+            )
+
+    def combine(p):
+        run(across[p, 0], across[p, 1])
+        for h in range(2):
+            span = pl.ds(h * n, n)
+            mixed = hidden_ref[span, :]
+            for e in range(8):
+                mixed = mixed + dot_f32(out_all[p][e, h], place[e, pl.ds(*SPANS[p])])
+            hidden_ref[span, :] = mixed
+
     loads[2].wait()
     for k in order:
-        p2[k] = product(2, k).astype(p2.dtype)
-        if k == order[0]:
-            entered()
-        a = send(p2.at[k, low], r1.at[k, 0], s1_send.at[k, 0], s1_recv.at[k, 0], up)
-        b = send(p2.at[k, high], r1.at[k, 1], s1_send.at[k, 1], s1_recv.at[k, 1], down)
-        steps[k] = (a, b)
-    tokens = slot_ref.shape[1]
-    down_rows = lax.broadcasted_iota(jnp.int32, (rows, tokens), 0)
-
-    def place_expert(e):
-        place[e] = (slot_ref[e : e + 1, :] == down_rows).astype(jnp.float32).astype(place.dtype)
-
-    lasts = {}
+        begin(0, k)
     loads[1].wait()
     loads[3].wait()
     for load in late:
         load.start()
     for k in order:
-        p1[k] = product(1, k).astype(p1.dtype)
-        c = send(p1.at[k, high], fin.at[k, 0, 1], s2_send.at[k, 0, 1], s2_recv.at[k, 0, 1], up)
-        pm[k] = product(3, k).astype(pm.dtype)
-        d = send(pm.at[k, low], fin.at[k, 1, 0], s2_send.at[k, 1, 0], s2_recv.at[k, 1, 0], down)
-        steps[k][0].wait_recv()
-        p1[k, low] = (p1[k, low].astype(jnp.float32) + r1[k, 0].astype(jnp.float32)).astype(p1.dtype)
-        e = send(p1.at[k, low], fin.at[k, 0, 0], s2_send.at[k, 0, 0], s2_recv.at[k, 0, 0], up)
-        steps[k][1].wait_recv()
-        pm[k, high] = (pm[k, high].astype(jnp.float32) + r1[k, 1].astype(jnp.float32)).astype(
-            pm.dtype
-        )
-        f = send(pm.at[k, high], fin.at[k, 1, 1], s2_send.at[k, 1, 1], s2_recv.at[k, 1, 1], down)
-        lasts[k] = (c, d, e, f)
+        middle(0, k)
+    for k in order:
+        begin(1, k)
     loads[0].wait()
+    end(0, 2)
+    end(0, 1)
+    one_hot(0)
+    one_hot(1)
+    end(0, 3)
+    middle(1, 2)
+    end(0, 0)
+    for k in (1, 3, 0):
+        middle(1, k)
     for load in late:
         load.wait()
     rep = lax.axis_index("rep")
@@ -629,74 +744,18 @@
     for q, (source, there) in enumerate(((first, last >= 0), (last, last > first))):
         block = came_ref[jnp.clip(source, 0, n_rep - 1)].astype(jnp.float32)
         arrived_ref[0, q] = jnp.where(there, block, 0.0).astype(arrived_ref.dtype)
-    for k in order:
-        whole = product(0, k)
-        for copy in lasts[k]:
-            copy.wait_recv()
-        whole = whole + jnp.concatenate(
-            [
-                fin[k, 0, 0].astype(jnp.float32) + fin[k, 1, 0].astype(jnp.float32),
-                fin[k, 0, 1].astype(jnp.float32) + fin[k, 1, 1].astype(jnp.float32),
-            ],
-            axis=0,
-        )
-        whole = whole.T
-        for e in range(2):
-            part = whole[e * (wide // 2) : (e + 1) * (wide // 2)]
-            turned[k, e] = part.astype(turned.dtype)
-            if k == 0:
-                tf[e] = part
-        first = 2 * lax.rem(pair + k, 4)
-        for e in range(2):
-            if k > 0:
-                there = dict(me, z=first + e)
-                send(
-                    turned.at[k, e],
-                    zr.at[2 * k + odd],
-                    z_send.at[2 * k + e],
-                    z_recv.at[2 * k + odd],
-                    there,
-                )
-        if k == 0:
-            there = dict(me, z=first + 1 - odd)
-            send(turned.at[0, 1 - odd], zr.at[odd], z_send.at[0], z_recv.at[odd], there)
-    total = tf[odd]
-    for k in order:
-        for e in range(2) if k > 0 else (0,):
-            slot = 2 * k + e if k > 0 else 1 - odd
-            remote(zr.at[slot], zr.at[slot], z_send.at[0], z_recv.at[slot], up).wait_recv()
-            total = total + zr[slot].astype(jnp.float32)
-    total = total * gate_ref[...]
-    n = out_own.shape[1]
-    across = []
-    for h in range(2):
-        out_own[h] = total[h * n : (h + 1) * n].astype(out_own.dtype)
-        across.append(
-            Gather(
-                me,
-                out_own.at[h],
-                lambda i, h=h: out_all.at[i, h],
-                xc,
-                kinds,
-                h,
-                (x_send, x_recv, x_own.at[h]),
-                8 * h,
-            )
-        )
-    for gather in across:
-        gather.step(gather.plan.pop(0))
-    for e in range(8):
-        place_expert(e)
-    run(*across)
-    for h in range(2):
-        span = pl.ds(h * n, n)
-        mixed = hidden_ref[span, :]
-        for e in range(8):
-            mixed = mixed + dot_f32(out_all[e, h], place[e])
-        o_ref[span, :] = mixed.astype(o_ref.dtype)
+    end(1, 2)
+    end(1, 1)
+    total(0)
+    end(1, 3)
+    end(1, 0)
+    combine(0)
+    total(1)
+    combine(1)
+    o_ref[...] = hidden_ref[...].astype(o_ref.dtype)
     for copy in copies:
         copy.wait_send()
-    for gather in across:
+    for gather in across.values():
         gather.finish()
 
 
@@ -722,27 +781,27 @@
             pltpu.VMEM((4, rows, width), kind),
             pltpu.VMEM((4, rows, width), kind),
             pltpu.VMEM((4, rows, width), kind),
-            pltpu.VMEM((4, 2, rows // 2, width), kind),
-            pltpu.VMEM((4, 2, 2, rows // 2, width), kind),
-            pltpu.VMEM((4, 2, width // 2, rows), kind),
-            pltpu.VMEM((2, width // 2, rows), jnp.float32),
-            pltpu.VMEM((8, width // 2, rows), kind),
+            pltpu.VMEM((4, rows, width), kind),
+            pltpu.VMEM((4, 2, rows, width), kind),
             pltpu.VMEM((8, rows, slots.shape[1]), kind),
-            pltpu.VMEM((2, width // 4, rows), kind),
-            pltpu.VMEM((8, 2, width // 4, rows), kind),
-            pltpu.SemaphoreType.DMA((4, 2)),
-            pltpu.SemaphoreType.DMA((4, 2)),
-            pltpu.SemaphoreType.DMA((4, 2, 2)),
-            pltpu.SemaphoreType.DMA((4, 2, 2)),
-            pltpu.SemaphoreType.DMA((8,)),
-            pltpu.SemaphoreType.DMA((8,)),
-            pltpu.SemaphoreType.DMA((16,)),
-            pltpu.SemaphoreType.DMA((16,)),
-            pltpu.SemaphoreType.DMA((2,)),
+            *[pltpu.VMEM((4, 2, width // 2, size), kind) for _, size in SPANS],
+            *[pltpu.VMEM((2, width // 2, size), jnp.float32) for _, size in SPANS],
+            *[pltpu.VMEM((8, width // 2, size), kind) for _, size in SPANS],
+            *[pltpu.VMEM((2, width // 4, size), kind) for _, size in SPANS],
+            *[pltpu.VMEM((8, 2, width // 4, size), kind) for _, size in SPANS],
+            pltpu.SemaphoreType.DMA((2, 4, 2)),
+            pltpu.SemaphoreType.DMA((2, 4, 2)),
+            pltpu.SemaphoreType.DMA((2, 4, 2, 2)),
+            pltpu.SemaphoreType.DMA((2, 4, 2, 2)),
+            pltpu.SemaphoreType.DMA((2, 8)),
+            pltpu.SemaphoreType.DMA((2, 8)),
+            pltpu.SemaphoreType.DMA((32,)),
+            pltpu.SemaphoreType.DMA((32,)),
+            pltpu.SemaphoreType.DMA((4,)),
             pltpu.SemaphoreType.DMA((7,)),
         ],
         compiler_params=pltpu.CompilerParams(
-            collective_id=collective_id, has_side_effects=True, vmem_limit_bytes=56 * 2**20
+            collective_id=collective_id, has_side_effects=True, vmem_limit_bytes=62 * 2**20
         ),
         name="down_scatter",
     )(act, w_down, gate, hidden, slots, came, mig_dest)
@@ -796,6 +855,7 @@
         capacity,
         1,
     )
+    w_in, u_all = lax.optimization_barrier((w_in, u_all))
     sums = jnp.sum(extra_all, axis=0)
     inverse = lax.rsqrt(sums[0] / D + EPSILON)
     gate_of_slot = 1.0 / (1.0 + jnp.exp(-sums[1] * inverse))

time: 178 us -> 160 us (0.90)
  local copies, waits for them, and re-layouts: 15 us -> 7.29 us
  Pallas kernels: 153 us -> 146 us
  matrix products: 6.52 us -> 2.69 us
    unnamed x37 -> x7, local copies, waits for them, and re-layouts: 15 us -> 7.29 us
    dot_general x1, matrix products: 6.52 us -> 2.69 us  [contract_first(): lax.dot_general(a, b, (((0,), (0,)), ((), ())), preferred_element_type=jn...]
    pallas_call x1, Pallas kernels: 85.4 us -> 81.6 us  [front(): pl.pallas_call(front_body, out_shape=[jax.ShapeDtypeStruct((32, mine, cap...]
    pallas_call x1, Pallas kernels: 67.8 us -> 64.5 us  [down_and_scatter(): pl.pallas_call(down_body, out_shape=[jax.ShapeDtypeStruct(hidden.shape, k...]
where the time goes in v4:
time: 160 us; the launch traced here: 159 us
  Pallas kernels  146 us (91%)
  local copies, waits for them, and re-layouts  7.29 us (5%)
  matrix products  2.69 us (2%)
  other arithmetic  2.48 us (2%)
    pallas_call x1, Pallas kernels, front(): pl.pallas_call(front_body, out_shape=[jax.ShapeDtypeStruct((32, mine, cap...  81.6 us
    pallas_call x1, Pallas kernels, down_and_scatter(): pl.pallas_call(down_body, out_shape=[jax.ShapeDtypeStruct(hidden.shape, k...  64.5 us
    unnamed x7, local copies, waits for them, and re-layouts  7.29 us

profile of v4, /device:TPU:1, one launch (start us, length us, event | category | flops | bytes accessed | tf_op | source)
XLA Modules:
  0.0 159.3 jit_solution(2366318115163848966)
XLA Ops:
  0.6 81.6 %front.1 = (bf16[32,192,384]{2,1,0:T(8,128)(2,1)}, f32[32,8,384]{2,1,0:T(8,128)}, f32[192,768]{1,0:T(8,128)}, bf16[32,2,128,128]{3,2,1,0:T(8,128)(2,1)}, s32[8,768]{1,0:T(8,128)}) custom-call(s32[24]{0:T(128)} %refs_0_.1, s32[4,24]{1,0:T(4,128)} %bitcast.30, f32[8,24]{1,0:T(8,128)} %bitcast.28, s32[32]{0:T(128)} %refs_3_.1, s32[32]{0:T(128)} %refs_4_.1, ...), custom_call_target="tpu_custom_call" | custom-call | tf_op jit(solution)/shard_map/front/pallas_call | solution.py:501
  82.3 0.0 slice-start
  82.3 1.1 reduce_sum.9
  83.4 0.6 add_divide_fusion
  84.0 0.0 slice-start.1
  84.0 4.0 %copy.20 = bf16[768,8,2,256]{3,1,2,0:T(8,128)(2,1)S(1)} copy(bf16[768,8,2,256]{3,2,1,0:T(2,128)(2,1)} %bitcast.21) | data formatting | bytes 12582912
  88.0 0.0 slice-done
  88.0 0.0 slice-done.1
  88.0 2.7 %convolution_multiply_fusion = f32[512,384]{0,1:T(8,128)S(1)} fusion(bf16[6144,512]{1,0:T(8,128)(2,1)S(1)} %bitcast.22, bf16[6144,384]{1,0:T(8,128)(2,1)S(1)} %bitcast.34, f32[384]{0:T(512)S(1)} %get-tuple-element.21), kind=kOutput, calls=%fused_computation | convolution fusion | flops 2416115712 | bytes 11798016 | tf_op jit(solution)/shard_map/dot_general | solution.py:811
  90.7 0.8 fusion.1.act_ref
  91.5 64.5 %down_scatter.1 = (bf16[192,768]{1,0:T(8,128)(2,1)}, bf16[1,2,2,128,128]{4,3,2,1,0:T(8,128)(2,1)}) custom-call(bf16[384,256]{1,0:T(8,128)(2,1)} %fusion.1.act_ref, bf16[256,6144]{1,0:T(8,128)(2,1)} %bitcast.23, f32[1,384]{1,0:T(1,128)} %get-tuple-element.20.gate_ref, f32[192,768]{1,0:T(8,128)} %get-tuple-element.15.hidden_hbm, ...), custom_call_target="tpu_custom_call" | custom-call | tf_op jit(solution)/shard_map/down_scatter/pallas_call | solution.py:768
  156.1 1.7 %copy.23 = bf16[768,192]{0,1:T(8,128)(2,1)} copy(bf16[768,192]{0,1:T(8,128)(2,1)} %bitcast.24) | data formatting | bytes 589824
  157.8 1.6 copy.24
  (1 shorter events, 0.0 us)
Async XLA Ops:
  82.3 5.7 %slice-start = ((s8[4718592]{0:T(1024)(128)(4,1)}), s8[524288]{0:T(1024)(128)(4,1)S(1)}, s32[]{:S(2)}) async-start(s8[4718592]{0:T(1024)(128)(4,1)} %bitcast.32), calls=%async_computation | async-start | bytes 1048576
  84.0 4.0 %slice-start.1 = ((s8[4718592]{0:T(1024)(128)(4,1)}), s8[4194304]{0:T(1024)(128)(4,1)S(1)}, s32[]{:S(2)}) async-start(s8[4718592]{0:T(1024)(128)(4,1)} %bitcast.32), calls=%async_computation.1 | async-start | bytes 8388608

commit v5 on v4

--- a/solution.py
+++ b/solution.py
@@ -285,7 +285,7 @@
 
 def front_body(*refs):
     hbm, outs, scratch = refs[:13], refs[13:18], refs[18:]
-    u_ref, extra_ref, hidden_ref, came_ref, slot_ref = outs
+    u_ref, factor_ref, hidden_ref, came_ref, slot_ref = outs
     local_refs, scratch = scratch[:13], scratch[13:]
     (
         lengths,
@@ -316,6 +316,7 @@
         part_all,
         rows_own,
         extra_own,
+        extra_all,
         send_sem,
         recv_sem,
         own_sem,
@@ -364,7 +365,7 @@
             )
             for n, piece in enumerate(PIECES)
         },
-        "extra": (extra_own, lambda i: extra_ref.at[i]),
+        "extra": (extra_own, lambda i: extra_all.at[i]),
     }
     g, base = {}, 0
     for n, (name, (dims, kinds, flip)) in enumerate(items.items()):
@@ -481,6 +482,10 @@
     move(10**6)
     for k in (*last, "going0", "going1"):
         g[k].own.wait()
+    sums = jnp.sum(extra_all[...], axis=0)
+    inverse = lax.rsqrt(sums[0:1] / D + EPSILON)
+    gate = 1.0 / (1.0 + jnp.exp(-sums[1:2] * inverse))
+    factor_ref[...] = jnp.concatenate([inverse, gate, sums[2:8] * 0.0], axis=0)
     for k in g:
         g[k].finish()
 
@@ -502,13 +507,13 @@
         front_body,
         out_shape=[
             jax.ShapeDtypeStruct((32, mine, capacity), kind),
-            jax.ShapeDtypeStruct((32, 8, capacity), jnp.float32),
+            jax.ShapeDtypeStruct((8, capacity), jnp.float32),
             jax.ShapeDtypeStruct((mine, tokens), jnp.float32),
             jax.ShapeDtypeStruct((32, *going), kind),
             jax.ShapeDtypeStruct((8, tokens), jnp.int32),
         ],
         in_specs=[pl.BlockSpec(memory_space=pltpu.HBM)] * 13,
-        out_specs=[anywhere, anywhere, vmem, anywhere, vmem],
+        out_specs=[anywhere, vmem, vmem, anywhere, vmem],
         scratch_shapes=[space(x.shape, x.dtype) for space, x in zip(spaces, inputs)]
         + [
             pltpu.VMEM((rows, split), kind),
@@ -524,6 +529,7 @@
             pltpu.VMEM((8, mine, tokens), kind),
             pltpu.VMEM((mine, capacity), kind),
             pltpu.VMEM((8, capacity), jnp.float32),
+            pltpu.VMEM((32, 8, capacity), jnp.float32),
             pltpu.SemaphoreType.DMA((total,)),
             pltpu.SemaphoreType.DMA((total,)),
             pltpu.SemaphoreType.DMA((len(items),)),
@@ -540,9 +546,9 @@
 
 
 def down_body(
-    act_ref,
+    raw_ref,
     w_hbm,
-    gate_ref,
+    factor_ref,
     hidden_hbm,
     slot_ref,
     came_hbm,
@@ -553,6 +559,7 @@
     hidden_ref,
     came_ref,
     dest_ref,
+    act_ref,
     p2,
     p1,
     pm,
@@ -564,8 +571,8 @@
     s1_send, s1_recv, s2_send, s2_recv, z_send, z_recv, x_send, x_recv, x_own, load_sem = rest[10:]
     turned, tf, zr, out_own, out_all = (rest[2 * k : 2 * k + 2] for k in range(5))
     me = coords()
-    xc, kinds = ("x", "c"), ("ring", "ring")
-    entered = greet(me, {"y": {1, 3}, "z": set(range(1, 8)), **partners(xc, kinds)})
+    xc, routes = ("x", "c"), (("ring", "ring"), ("two", "ring"))
+    entered = greet(me, {"y": {1, 3}, "z": set(range(1, 8)), **partners(xc, routes[1])})
     group = w_ref.shape[1] // 4
     loads = {}
     for k, step in enumerate((2, 1, 3, 0)):
@@ -678,7 +685,7 @@
                     zr[p].at[slot], zr[p].at[slot], z_send.at[p, 0], z_recv.at[p, slot], up
                 ).wait_recv()
                 found = found + zr[p][slot].astype(jnp.float32)
-        found = found * gate_ref[:, pl.ds(*SPANS[p])]
+        found = found * factor_ref[1:2, pl.ds(*SPANS[p])]
         for h in range(2):
             out_own[p][h] = found[h * n : (h + 1) * n].astype(out_own[p].dtype)
             gather = Gather(
@@ -686,7 +693,7 @@
                 out_own[p].at[h],
                 lambda i, h=h: out_all[p].at[i, h],
                 xc,
-                kinds,
+                routes[p],
                 h,
                 (x_send, x_recv, x_own.at[2 * p + h]),
                 8 * (2 * p + h),
@@ -711,6 +718,11 @@
                 mixed = mixed + dot_f32(out_all[p][e, h], place[e, pl.ds(*SPANS[p])])
             hidden_ref[span, :] = mixed
 
+    inverse = jnp.broadcast_to(factor_ref[0:1, :], factor_ref.shape).T[:, :1]
+    depth = act_ref.shape[1]
+    gate = raw_ref[:, :depth] * inverse
+    act = gate * (1.0 / (1.0 + jnp.exp(-gate))) * (raw_ref[:, depth:] * inverse)
+    act_ref[...] = act.astype(act_ref.dtype)
     loads[2].wait()
     for k in order:
         begin(0, k)
@@ -759,12 +771,12 @@
         gather.finish()
 
 
-def down_and_scatter(act, w_down, gate, hidden, slots, came, mig_dest, collective_id):
-    rows, depth = act.shape
+def down_and_scatter(raw, w_down, factors, hidden, slots, came, mig_dest, collective_id):
+    rows, depth = raw.shape[0], w_down.shape[0]
     width = w_down.shape[1] // 16
     vmem = pl.BlockSpec(memory_space=pltpu.VMEM)
     hbm = pl.BlockSpec(memory_space=pltpu.HBM)
-    kind = act.dtype
+    kind = w_down.dtype
     return pl.pallas_call(
         down_body,
         out_shape=[
@@ -778,6 +790,7 @@
             pltpu.VMEM(hidden.shape, hidden.dtype),
             pltpu.VMEM(came.shape, kind),
             pltpu.SMEM(mig_dest.shape, mig_dest.dtype),
+            pltpu.VMEM((rows, depth), kind),
             pltpu.VMEM((4, rows, width), kind),
             pltpu.VMEM((4, rows, width), kind),
             pltpu.VMEM((4, rows, width), kind),
@@ -804,7 +817,23 @@
             collective_id=collective_id, has_side_effects=True, vmem_limit_bytes=62 * 2**20
         ),
         name="down_scatter",
-    )(act, w_down, gate, hidden, slots, came, mig_dest)
+    )(raw, w_down, factors, hidden, slots, came, mig_dest)
+
+
+def finish_body(mixed_ref, arrived_ref, mixed_out, arrived_out):
+    mixed_out[...] = mixed_ref[...]
+    arrived_out[...] = arrived_ref[...]
+
+
+def finish(mixed, arrived):
+    vmem = pl.BlockSpec(memory_space=pltpu.VMEM)
+    return pl.pallas_call(
+        finish_body,
+        out_shape=[jax.ShapeDtypeStruct(x.shape, x.dtype) for x in (mixed, arrived)],
+        in_specs=[vmem] * 2,
+        out_specs=[vmem] * 2,
+        name="finish",
+    )(mixed, arrived)
 
 
 def contract_first(a, b, **kw):
@@ -836,7 +865,7 @@
     ff = w_in.shape[3]
     choice = expert_choice.T
     rows = query.shape[0]
-    u_all, extra_all, hidden, came, slots = front(
+    u_all, factors, hidden, came, slots = front(
         [
             lengths,
             precision.T,
@@ -856,15 +885,11 @@
         1,
     )
     w_in, u_all = lax.optimization_barrier((w_in, u_all))
-    sums = jnp.sum(extra_all, axis=0)
-    inverse = lax.rsqrt(sums[0] / D + EPSILON)
-    gate_of_slot = 1.0 / (1.0 + jnp.exp(-sums[1] * inverse))
-    gate_up = contract_first(w_in[0].reshape(D, 2 * ff), u_all.reshape(D, capacity))
-    gate_up = gate_up * inverse[None, :]
-    act = (jax.nn.silu(gate_up[:ff]) * gate_up[ff:]).astype(jnp.bfloat16)
+    gate_up = contract_first(u_all.reshape(D, capacity), w_in[0].reshape(D, 2 * ff))
     mixed, arrived = down_and_scatter(
-        act.T, w_down[0], gate_of_slot[None], hidden, slots, came, mig_dest, 2
-    )
+        gate_up, w_down[0], factors, hidden, slots, came, mig_dest, 2
+    )
+    mixed, arrived = finish(mixed, arrived)
     return (mixed.T, arrived)
 
 

time: 160 us -> 156 us (0.975)
  local copies, waits for them, and re-layouts: 7.29 us -> 4.14 us
  other arithmetic: 2.48 us -> 0 us
    unnamed x7 -> x3, local copies, waits for them, and re-layouts: 7.29 us -> 4.14 us
    pallas_call x0 -> x1, Pallas kernels: none -> 1.77 us  [finish(): pl.pallas_call(finish_body, out_shape=[jax.ShapeDtypeStruct(x.shape, x.dt...]
where the time goes in v5:
time: 156 us; the launch traced here: 155 us
  Pallas kernels  147 us (94%)
  local copies, waits for them, and re-layouts  4.14 us (3%)
  matrix products  3.51 us (2%)
    pallas_call x1, Pallas kernels, front(): pl.pallas_call(front_body, out_shape=[jax.ShapeDtypeStruct((32, mine, cap...  81.8 us
    pallas_call x1, Pallas kernels, down_and_scatter(): pl.pallas_call(down_body, out_shape=[jax.ShapeDtypeStruct(hidden.shape, k...  63.5 us
    unnamed x3, local copies, waits for them, and re-layouts  4.14 us
    dot_general x1, matrix products, contract_first(): lax.dot_general(a, b, (((0,), (0,)), ((), ())), preferred_element_type=jn...  3.51 us

profile of v5, /device:TPU:1, one launch (start us, length us, event | category | flops | bytes accessed | tf_op | source)
XLA Modules:
  0.0 155.4 jit_solution(176018093827937587)
XLA Ops:
  0.6 81.8 %front.1 = (bf16[32,192,384]{2,1,0:T(8,128)(2,1)}, f32[8,384]{1,0:T(8,128)}, f32[192,768]{1,0:T(8,128)}, bf16[32,2,128,128]{3,2,1,0:T(8,128)(2,1)}, s32[8,768]{1,0:T(8,128)}) custom-call(s32[24]{0:T(128)} %refs_0_.1, s32[4,24]{1,0:T(4,128)} %bitcast.28, f32[8,24]{1,0:T(8,128)} %bitcast.26, s32[32]{0:T(128)} %refs_3_.1, s32[32]{0:T(128)} %refs_4_.1, ...), custom_call_target="tpu_custom_call" | custom-call | tf_op jit(solution)/shard_map/front/pallas_call | solution.py:506
  82.4 0.0 copy-start
  82.4 4.0 %copy.18 = bf16[768,8,2,256]{3,1,2,0:T(8,128)(2,1)S(1)} copy(bf16[768,8,2,256]{3,2,1,0:T(2,128)(2,1)} %bitcast.21) | data formatting | bytes 12582912
  86.4 0.1 copy-done
  86.5 3.5 %fusion.raw_ref = f32[384,512]{1,0:T(8,128)} fusion(bf16[6144,384]{1,0:T(8,128)(2,1)S(1)} %bitcast.20, bf16[6144,512]{1,0:T(8,128)(2,1)S(1)} %bitcast.19), kind=kOutput, calls=%fused_computation | convolution fusion | flops 2415919104 | bytes 11796480 | tf_op jit(solution)/shard_map/dot_general | solution.py:840
  90.1 63.5 %down_scatter.1 = (bf16[192,768]{1,0:T(8,128)(2,1)}, bf16[1,2,2,128,128]{4,3,2,1,0:T(8,128)(2,1)}) custom-call(f32[384,512]{1,0:T(8,128)} %fusion.raw_ref, bf16[256,6144]{1,0:T(8,128)(2,1)} %bitcast.22, f32[8,384]{1,0:T(8,128)} %get-tuple-element.16.factor_ref, f32[192,768]{1,0:T(8,128)} %get-tuple-element.17.hidden_hbm, ...), custom_call_target="tpu_custom_call" | custom-call | tf_op jit(solution)/shard_map/down_scatter/pallas_call | solution.py:780
  153.6 1.8 %finish.1 = (bf16[192,768]{1,0:T(8,128)(2,1)}, bf16[1,2,2,128,128]{4,3,2,1,0:T(8,128)(2,1)}) custom-call(bf16[192,768]{1,0:T(8,128)(2,1)} %get-tuple-element.20.mixed_ref, bf16[1,2,2,128,128]{4,3,2,1,0:T(8,128)(2,1)} %get-tuple-element.21.arrived_ref), custom_call_target="tpu_custom_call" | custom-call | tf_op jit(solution)/shard_map/finish/pallas_call | solution.py:830
Async XLA Ops:
  82.4 4.2 %copy-start = (bf16[32,192,384]{2,1,0:T(8,128)(2,1)S(1)}, bf16[32,192,384]{2,1,0:T(8,128)(2,1)}, u32[]{:S(2)}) copy-start(bf16[32,192,384]{2,1,0:T(8,128)(2,1)} %get-tuple-element.14) | copy-start | bytes 14155780

commit v6 on v5

--- a/solution.py
+++ b/solution.py
@@ -477,7 +477,7 @@
     )
     for cost, n, event in todo:
         if cost > 8:
-            move(cost + 2)
+            move(cost - 2)
         g[last[n]].step(event)
     move(10**6)
     for k in (*last, "going0", "going1"):
@@ -571,7 +571,7 @@
     s1_send, s1_recv, s2_send, s2_recv, z_send, z_recv, x_send, x_recv, x_own, load_sem = rest[10:]
     turned, tf, zr, out_own, out_all = (rest[2 * k : 2 * k + 2] for k in range(5))
     me = coords()
-    xc, routes = ("x", "c"), (("ring", "ring"), ("two", "ring"))
+    xc, routes = ("x", "c"), (("two", "ring"), ("two", "ring"))
     entered = greet(me, {"y": {1, 3}, "z": set(range(1, 8)), **partners(xc, routes[1])})
     group = w_ref.shape[1] // 4
     loads = {}

time: 156 us -> 152 us (0.974)
  Pallas kernels: 147 us -> 144 us
    pallas_call x1, Pallas kernels: 63.5 us -> 60.3 us  [down_and_scatter(): pl.pallas_call(down_body, out_shape=[jax.ShapeDtypeStruct(hidden.shape, k...]
where the time goes in v6:
time: 152 us
  Pallas kernels  144 us (95%)
  local copies, waits for them, and re-layouts  4.14 us (3%)
  matrix products  3.51 us (2%)
    pallas_call x1, Pallas kernels, front(): pl.pallas_call(front_body, out_shape=[jax.ShapeDtypeStruct((32, mine, cap...  81.8 us
    pallas_call x1, Pallas kernels, down_and_scatter(): pl.pallas_call(down_body, out_shape=[jax.ShapeDtypeStruct(hidden.shape, k...  60.3 us
    unnamed x3, local copies, waits for them, and re-layouts  4.14 us
    dot_general x1, matrix products, contract_first(): lax.dot_general(a, b, (((0,), (0,)), ((), ())), preferred_element_type=jn...  3.51 us

profile of v6, /device:TPU:1, one launch (start us, length us, event | category | flops | bytes accessed | tf_op | source)
XLA Modules:
  0.0 152.2 jit_solution(10914713254866583924)
XLA Ops:
  0.6 81.8 %front.1 = (bf16[32,192,384]{2,1,0:T(8,128)(2,1)}, f32[8,384]{1,0:T(8,128)}, f32[192,768]{1,0:T(8,128)}, bf16[32,2,128,128]{3,2,1,0:T(8,128)(2,1)}, s32[8,768]{1,0:T(8,128)}) custom-call(s32[24]{0:T(128)} %refs_0_.1, s32[4,24]{1,0:T(4,128)} %bitcast.28, f32[8,24]{1,0:T(8,128)} %bitcast.26, s32[32]{0:T(128)} %refs_3_.1, s32[32]{0:T(128)} %refs_4_.1, ...), custom_call_target="tpu_custom_call" | custom-call | tf_op jit(solution)/shard_map/front/pallas_call | solution.py:506
  82.4 0.0 copy-start
  82.5 4.0 %copy.18 = bf16[768,8,2,256]{3,1,2,0:T(8,128)(2,1)S(1)} copy(bf16[768,8,2,256]{3,2,1,0:T(2,128)(2,1)} %bitcast.21) | data formatting | bytes 12582912
  86.5 0.1 copy-done
  86.6 3.5 %fusion.raw_ref = f32[384,512]{1,0:T(8,128)} fusion(bf16[6144,384]{1,0:T(8,128)(2,1)S(1)} %bitcast.20, bf16[6144,512]{1,0:T(8,128)(2,1)S(1)} %bitcast.19), kind=kOutput, calls=%fused_computation | convolution fusion | flops 2415919104 | bytes 11796480 | tf_op jit(solution)/shard_map/dot_general | solution.py:840
  90.1 60.3 %down_scatter.1 = (bf16[192,768]{1,0:T(8,128)(2,1)}, bf16[1,2,2,128,128]{4,3,2,1,0:T(8,128)(2,1)}) custom-call(f32[384,512]{1,0:T(8,128)} %fusion.raw_ref, bf16[256,6144]{1,0:T(8,128)(2,1)} %bitcast.22, f32[8,384]{1,0:T(8,128)} %get-tuple-element.16.factor_ref, f32[192,768]{1,0:T(8,128)} %get-tuple-element.17.hidden_hbm, ...), custom_call_target="tpu_custom_call" | custom-call | tf_op jit(solution)/shard_map/down_scatter/pallas_call | solution.py:780
  150.4 1.8 %finish.1 = (bf16[192,768]{1,0:T(8,128)(2,1)}, bf16[1,2,2,128,128]{4,3,2,1,0:T(8,128)(2,1)}) custom-call(bf16[192,768]{1,0:T(8,128)(2,1)} %get-tuple-element.20.mixed_ref, bf16[1,2,2,128,128]{4,3,2,1,0:T(8,128)(2,1)} %get-tuple-element.21.arrived_ref), custom_call_target="tpu_custom_call" | custom-call | tf_op jit(solution)/shard_map/finish/pallas_call | solution.py:830
Async XLA Ops:
  82.4 4.2 %copy-start = (bf16[32,192,384]{2,1,0:T(8,128)(2,1)S(1)}, bf16[32,192,384]{2,1,0:T(8,128)(2,1)}, u32[]{:S(2)}) copy-start(bf16[32,192,384]{2,1,0:T(8,128)(2,1)} %get-tuple-element.14) | copy-start | bytes 14155780
